TPU v7x, 32 devices: a whole 2x2x4 slice. The times are simulated.
32 devices in a mesh: ctx: 16 (over z, x, core), dp: 2 (over y).
Axes of the slice: x: 2, y: 2, z: 4, core: 2. Of those that a mesh axis runs over, the one named last changes fastest.
Arguments:
- query_proj: bfloat16 [2, 2048, 1024], P('dp', 'ctx'), may hold values from -6 to 6
- key_proj: bfloat16 [2, 2048, 1024], P('dp', 'ctx'), may hold values from -6 to 6
- value_proj: bfloat16 [2, 2048, 1024], P('dp', 'ctx'), may hold values from -6 to 6
- grad_out: bfloat16 [2, 2048, 4096], P('dp', 'ctx'), may hold values from -6 to 6
- out_weight: bfloat16 [1024, 4096], P('ctx'), may hold values from -0.1875 to 0.1875
- short_taps: float32 [3, 1024, 7], replicated, may hold values from -2 to 2
- residues: float32 [1024, 16], replicated, may hold values from -1.5 to 1.5
- decay_rate: float32 [1024, 16], replicated, may hold values from 0.00012207031 to 0.05
Outputs:
- grad_query: bfloat16 [2, 2048, 1024], P('dp', 'ctx')
- grad_key: bfloat16 [2, 2048, 1024], P('dp', 'ctx')
- grad_value: bfloat16 [2, 2048, 1024], P('dp', 'ctx')
- weight_grad: float32 [1024, 4096], P('ctx')
- taps_grad: float32 [3, 1024, 7], replicated
- residue_grad: float32 [1024, 16], replicated
All inputs are finite; a program needn't handle non-finite values.
Results may differ from a plain program's by a relative error of at most 0.0075.
Values may be sent and summed in bfloat16 or wider, within the bound.
A program may use at most 192 MiB of HBM per device.

v0:
```python
import math

import jax
import jax.numpy as jnp
from jax import lax
from jax.sharding import PartitionSpec as P

HIGH = lax.Precision.HIGHEST


def passed_along(value, axis, steps):
    count = lax.axis_size(axis)
    first, last = (max(0, -steps), min(count, count - steps))
    return lax.ppermute(value, axis, [(source, source + steps) for source in range(first, last)])


def entering(x, axis, combine, identity, reverse):
    length, position = (lax.axis_size(axis), lax.axis_index(axis))
    everything = jax.tree.map(lambda part: lax.all_gather(part, axis), x)
    start = jax.tree.map(
        lambda part, zero: jnp.broadcast_to(jnp.asarray(zero, part.dtype), part.shape), x, identity
    )

    def hop(k, before):
        at = length - 1 - k if reverse else k
        reached = at > position if reverse else at < position
        new = combine(before, jax.tree.map(lambda part: part[at], everything))
        return jax.tree.map(lambda a, b: jnp.where(reached, a, b), new, before)

    return lax.fori_loop(0, length, hop, start)


def for_sending(x):
    return jax.tree.map(lambda a: a.astype(jnp.bfloat16) if a.dtype == jnp.float32 else a, x)


def local_modes(mixed, grad_filtered, rate, coef):
    tokens, width = mixed.shape
    sub = math.gcd(tokens, 64)
    blocks = tokens // sub
    offsets = jnp.arange(sub, dtype=jnp.float32)
    rows_index = jnp.arange(sub)
    lower_mask = rows_index[:, None] >= rows_index[None, :]
    upper_mask = rows_index[:, None] <= rows_index[None, :]
    lag_index = jnp.maximum(rows_index[:, None] - rows_index[None, :], 0)
    decay_lag = jnp.exp(-rate[:, None, :] * offsets[None, :, None])
    kernel = jnp.einsum("mc,mdc->dc", coef, decay_lag, precision=HIGH)
    toeplitz = jnp.where(lower_mask[:, :, None], kernel[lag_index], 0.0)
    mixed_blocks = mixed.reshape(blocks, sub, width)
    grad_blocks = grad_filtered.reshape(blocks, sub, width)
    filt_inner = jnp.einsum("bjc,njc->nbc", toeplitz, mixed_blocks, precision=HIGH)
    adj_inner = jnp.einsum("jbc,njc->nbc", toeplitz, grad_blocks, precision=HIGH)
    to_end = jnp.exp(-rate[:, None, :] * (sub - 1.0 - offsets)[None, :, None])
    ends_block = jnp.einsum("njc,mjc->nmc", mixed_blocks, to_end, precision=HIGH)
    firsts_block = jnp.einsum("njc,mjc->nmc", grad_blocks, decay_lag, precision=HIGH)
    places = jnp.arange(blocks, dtype=jnp.float32)
    diff = places[:, None] - places[None, :]
    carry_mat = jnp.where(
        (diff >= 0)[:, :, None, None],
        jnp.exp(-(rate * sub)[None, None] * jnp.maximum(diff, 0.0)[:, :, None, None]),
        0.0,
    )
    after = jnp.einsum("ikmc,kmc->imc", carry_mat, ends_block, precision=HIGH)
    before = jnp.einsum("kimc,kmc->imc", carry_mat, firsts_block, precision=HIGH)
    correlation = jnp.einsum("nbc,njc->bjc", mixed_blocks, grad_blocks, precision=HIGH)
    correlation = jnp.where(upper_mask[:, :, None], correlation, 0.0)
    growth = jnp.exp(rate[:, None, :] * offsets[None, :, None])
    partial_y = jnp.einsum("bjc,mbc->mjc", correlation, growth, precision=HIGH)
    within = jnp.sum(partial_y * decay_lag, axis=1)
    return (filt_inner, adj_inner, ends_block, after, before, within)


def chain_pair(earlier, later):
    return (earlier[0] * later[0], later[0] * earlier[1] + later[1])


def shards(
    query_proj, key_proj, value_proj, grad_out, out_weight, short_taps, residues, decay_rate
):
    stacked = jnp.stack([query_proj[0], key_proj[0], value_proj[0]])
    tokens = stacked.shape[1]
    width = stacked.shape[2]
    behind = passed_along(stacked[:, tokens - 6 :, :], "ctx", 1)
    widened = jnp.concatenate([behind, stacked], axis=1).astype(jnp.float32)
    shaped = jnp.zeros((3, tokens, width), jnp.float32)
    for lag in range(7):
        shaped = shaped + short_taps[:, None, :, lag] * widened[:, 6 - lag : 6 - lag + tokens, :]
    shaped_q, shaped_k, shaped_v = (shaped[0], shaped[1], shaped[2])
    mixed = shaped_k * shaped_v
    out_rows = grad_out[0]
    upstream = lax.dot_general(
        out_rows,
        lax.all_gather(out_weight, "ctx", axis=0, tiled=True),
        (((1,), (1,)), ((), ())),
        preferred_element_type=jnp.float32,
    )
    grad_filtered = upstream * shaped_q
    rate_t = decay_rate.T
    norm_t = jnp.sqrt(-jnp.expm1(-2.0 * rate_t))
    coef_t = residues.T * norm_t
    filt_inner, adj_inner, ends_block, after, before, within = local_modes(
        mixed, grad_filtered, rate_t, coef_t
    )
    blocks = ends_block.shape[0]
    sub = tokens // blocks
    ends = after[blocks - 1]
    firsts = before[0]
    span = jnp.exp(-rate_t * tokens)
    unit = (jnp.ones_like(span), jnp.zeros_like(ends))
    incoming = entering((span, ends), "ctx", chain_pair, unit, False)[1]
    outgoing = entering((span, firsts), "ctx", chain_pair, unit, True)[1]
    blank_row = jnp.zeros_like(ends)[None]
    places = jnp.arange(blocks, dtype=jnp.float32)[:, None, None]
    span_sub = (rate_t * sub)[None]
    starts = (
        jnp.concatenate([blank_row, after[: blocks - 1]], axis=0)
        + jnp.exp(-span_sub * places) * incoming[None]
    )
    back_starts = (
        jnp.concatenate([before[1:], blank_row], axis=0)
        + jnp.exp(-span_sub * (blocks - 1.0 - places)) * outgoing[None]
    )
    offsets = jnp.arange(sub, dtype=jnp.float32)[None, :, None]
    apply_fore = coef_t[:, None, :] * jnp.exp(-rate_t[:, None, :] * (offsets + 1.0))
    apply_back = coef_t[:, None, :] * jnp.exp(-rate_t[:, None, :] * (sub - offsets))
    filtered = (
        filt_inner + jnp.einsum("nmc,mbc->nbc", starts, apply_fore, precision=HIGH)
    ).reshape(tokens, width)
    grad_mixed = (
        adj_inner + jnp.einsum("nmc,mbc->nbc", back_starts, apply_back, precision=HIGH)
    ).reshape(tokens, width)
    residue_part = norm_t * (within + jnp.exp(-rate_t) * jnp.sum(back_starts * ends_block, axis=0))
    gated = (shaped_q * filtered).astype(jnp.bfloat16)
    grad_shaped = jnp.stack([upstream * filtered, grad_mixed * shaped_v, grad_mixed * shaped_k])
    ahead = passed_along(for_sending(grad_shaped[:, :6, :]), "ctx", -1)
    longer = jnp.concatenate([grad_shaped, ahead], axis=1)
    streams = jnp.zeros((3, tokens, width), jnp.float32)
    for lag in range(7):
        streams = streams + short_taps[:, None, :, lag] * longer[:, lag : lag + tokens, :]
    streams = streams.astype(jnp.bfloat16)
    taps_part = jnp.stack(
        [
            jnp.sum(grad_shaped * widened[:, 6 - lag : 6 - lag + tokens, :], axis=1)
            for lag in range(7)
        ],
        axis=1,
    )
    taps_total, residue_total = lax.psum((taps_part, residue_part), ("ctx", "dp"))
    taps_grad = jnp.swapaxes(taps_total, 1, 2)
    residue_grad = residue_total.T
    summed = lax.psum_scatter(
        lax.dot_general(
            gated, out_rows, (((0,), (0,)), ((), ())), preferred_element_type=jnp.float32
        ),
        "ctx",
        scatter_dimension=0,
        tiled=True,
    )
    weight_grad = lax.psum(summed.astype(jnp.bfloat16), "dp").astype(jnp.float32)
    return (
        streams[0][None],
        streams[1][None],
        streams[2][None],
        weight_grad,
        taps_grad,
        residue_grad,
    )


def solution(mesh):
    placed = (
        P("dp", "ctx", None),
        P("dp", "ctx", None),
        P("dp", "ctx", None),
        P("dp", "ctx", None),
        P("ctx", None),
        P(),
        P(),
        P(),
    )
    return jax.shard_map(
        shards,
        mesh=mesh,
        in_specs=placed,
        out_specs=(
            P("dp", "ctx", None),
            P("dp", "ctx", None),
            P("dp", "ctx", None),
            P("ctx", None),
            P(),
            P(),
        ),
        check_vma=False,
    )
```

profile of v0, /device:TPU:8, one launch (start us, length us, event | category | flops | bytes accessed | tf_op | source)
XLA Modules:
  0.0 670.6 jit_solution(622997670286050964)
XLA Ops:
  10.3 1.9 collective-permute-start
  13.5 3.1 collective-permute-done
  16.8 1.3 multiply_add_fusion
  19.1 2.2 copy.112
  21.2 16.2 %fusion.21 = f32[1024,16,2]{1,2,0:T(2,128)} fusion(f32[2,64,1024]{1,0,2:T(2,128)} %copy.112, f32[64]{0:T(128)S(1)} %iota_subtract_fusion.3, f32[16,1024]{0,1:T(8,128)S(1)} %copy.110), kind=kOutput, calls=%fused_computation.29 | convolution fusion | flops 26214400 | bytes 721152 | tf_op jit(solution)/shard_map/njc,mjc->nmc/dot_general | solution.py:54
  37.4 2.0 copy.166
  40.4 1.3 copy.147
  41.7 3.4 fusion.79
  45.2 1.8 copy.118
  50.8 16.3 %multiply_reduce_fusion = f32[1024,64]{1,0:T(8,128)} fusion(f32[1024,16]{1,0:T(8,128)} %copy.165, f32[16,1024]{0,1:T(8,128)S(1)} %copy.110), kind=kLoop, calls=%fused_computation.21 | loop fusion | flops 3080192 | bytes 393216
  67.1 1.2 copy.138
  68.9 1.4 reshape.139
  71.1 18.5 %gather_fusion = f32[4096,1024]{1,0:T(8,128)} fusion(f32[64,1024]{1,0:T(8,128)S(1)} %bitcast.138, s32[4096]{0:T(1024)S(1)} %broadcast_clamp_fusion), kind=kCustom, calls=%fused_computation | custom fusion | bytes 33570816 | tf_op jit(solution)/shard_map/gather | solution.py:48
  89.6 31.0 %copy.111 = f32[64,64,1024]{0,1,2:T(8,128)} copy(f32[64,64,1024]{2,1,0:T(8,128)} %bitcast.139) | data formatting | bytes 33554432 | tf_op jit(solution)/shard_map/gather | solution.py:48
  120.6 31.0 %fusion.5 = f32[1024,2,64]{2,1,0:T(2,128)} fusion(f32[2,64,1024]{1,0,2:T(2,128)} %copy.112, f32[64,64,1024]{0,1,2:T(8,128)} %copy.111, pred[64,64]{0,1:T(8,128)(4,1)S(1)} %iota_compare_fusion.1), kind=kOutput, calls=%fused_computation.11 | convolution fusion | flops 104857600 | bytes 17829888 | tf_op jit(solution)/shard_map/bjc,njc->nbc/dot_general | solution.py:51
  151.6 2.3 copy.114
  153.9 15.0 %while.30 = (s32[]{:T(128)}, f32[16,1024]{1,0:T(8,128)S(1)}, s32[]{:T(128)}, f32[16,16,1024]{2,1,0:T(8,128)}, f32[16,16,1024]{2,1,0:T(8,128)}, /*index=5*/s32[]{:T(128)}, s32[]{:T(128)}) while((s32[]{:T(128)}, f32[16,1024]{1,0:T(8,128)S(1)}, s32[]{:T(128)}, f32[16,16,1024]{2,1,0:T(8,128)}, f32[16,16,1024]{2,1,0:T(8,128)}, ...), condition=%wide.region_1.2_spmd.clone, body=%wide.region_0.1_spmd.clone.sunk | while | flops 65540 | bytes 262253 | solution.py:30
  169.9 13.1 %fusion.24 = f32[1024,64,2]{1,2,0:T(2,128)} fusion(f32[64]{0:T(128)S(1)} %iota_add_fusion, f32[16,1024]{0,1:T(8,128)} %copy.115, f32[16,1024]{0,1:T(8,128)S(1)} %copy.110, f32[1,16,1024]{1,0,2:T(1,128)} %get-tuple-element.354, f32[16,1024]{0,1:T(8,128)} %copy.119, f32[16,1024]{0,1:T(8,128)} %copy.117), kind=kOutput, calls=%fused_computation.32 | convolution fusion | flops 27361280 | bytes 852224 | tf_op jit(solution)/shard_map/nmc,mbc->nbc/dot_general | solution.py:127
  183.0 2.5 copy.120
  185.5 1.3 bitcast_add_fusion.2
  186.8 7.2 %bitcast_multiply_fusion.8 = (f32[128,1024]{1,0:T(8,128)}, f32[128,1024]{1,0:T(8,128)}) fusion(f32[2,64,1024]{2,1,0:T(8,128)S(1)} %bitcast_add_fusion.2, f32[3,128,1024]{2,1,0:T(8,128)S(1)} %multiply_add_fusion, bf16[1024,4096]{1,0:T(8,128)(2,1)} %all-gather.6.cloned.1.call-done, bf16[1,128,4096]{2,1,0:T(8,128)(2,1)S(1)} %copy-done), kind=kOutput, calls=%fused_computation.94 | convolution fusion | flops 1074003968 | bytes 11534336 | tf_op jit(solution)/shard_map/dot_general | solution.py:91
  194.0 2.2 copy.121
  196.2 16.2 %fusion.48 = f32[16,1024,2]{0,2,1:T(2,128)} fusion(f32[2,64,1024]{1,0,2:T(2,128)} %copy.121, f32[16,1024]{0,1:T(8,128)} %copy-done.10), kind=kOutput, calls=%fused_computation.71 | convolution fusion | flops 26214400 | bytes 720896 | tf_op jit(solution)/shard_map/njc,mjc->nmc/dot_general | solution.py:55
  212.4 1.4 copy.167
  213.9 1.3 copy.156
  215.2 3.4 fusion.80
  218.6 1.8 copy.124
  220.5 56.8 %fusion.55 = f32[2,64,1024]{1,0,2:T(2,128)} fusion(f32[2,64,1024]{1,0,2:T(2,128)} %copy.121, f32[64,64,1024]{0,1,2:T(8,128)} %copy.111, pred[64,64]{0,1:T(8,128)(4,1)S(1)} %iota_compare_fusion.1), kind=kOutput, calls=%fused_computation.74 | convolution fusion | flops 104857600 | bytes 17829888 | tf_op jit(solution)/shard_map/jbc,njc->nbc/dot_general | solution.py:52
  277.3 15.0 %while.31 = (s32[]{:T(128)}, f32[16,1024]{1,0:T(8,128)S(1)}, s32[]{:T(128)}, f32[16,16,1024]{2,1,0:T(8,128)}, f32[16,16,1024]{2,1,0:T(8,128)}, /*index=5*/s32[]{:T(128)}, s32[]{:T(128)}, s32[]{:T(128)}, s32[]{:T(128)}) while((s32[]{:T(128)}, f32[16,1024]{1,0:T(8,128)S(1)}, s32[]{:T(128)}, f32[16,16,1024]{2,1,0:T(8,128)}, ...), condition=%wide.region_3.4_spmd.clone, body=%wide.region_2.3_spmd.clone.sunk | while | flops 65544 | bytes 262315 | solution.py:30
  293.3 13.3 %fusion.52 = f32[2,64,1024]{1,0,2:T(2,128)} fusion(f32[2,64,1024]{1,0,2:T(2,128)} %fusion.55, f32[64]{0:T(128)S(1)} %iota_subtract_fusion.2, f32[16,1024]{0,1:T(8,128)} %copy.115, f32[16,1024]{0,1:T(8,128)} %copy-done.10, f32[1,16,1024]{1,0,2:T(1,128)} %get-tuple-element.356, f32[16,1024]{0,1:T(8,128)} %copy.125, f32[16,1024]{0,1:T(8,128)} %copy.117, ...), kind=kOutput, calls=%fused_computation.73 | convolution fusion | flops 27492352 | bytes 1376520 | tf_op jit(solution)/shard_map/nmc,mbc->nbc/dot_general | solution.py:130
  306.6 2.1 copy.126
  308.8 2.2 bitcast_multiply_fusion.6
  310.9 8.1 %fusion.59 = f32[1024,4096]{1,0:T(8,128)} fusion(bf16[128,1024]{1,0:T(8,128)(2,1)S(1)} %get-tuple-element.352, bf16[1,128,4096]{2,1,0:T(8,128)(2,1)S(1)} %copy-done), kind=kOutput, calls=%fused_computation.77 | convolution fusion | flops 1073741824 | bytes 18087936 | tf_op jit(solution)/shard_map/dot_general | solution.py:152
  320.9 56.6 %fusion.83 = f32[1024,64,64]{2,1,0:T(8,128)} fusion(f32[2,64,1024]{1,0,2:T(2,128)S(1)} %copy-done.4, f32[2,64,1024]{1,0,2:T(2,128)S(1)} %copy-done.3), kind=kOutput, calls=%fused_computation.139 | convolution fusion | flops 100663296 | bytes 17825792 | tf_op jit(solution)/shard_map/nbc,njc->bjc/dot_general | solution.py:65
  377.6 57.4 %fusion.13 = f32[16,1024]{0,1:T(8,128)} fusion(f32[16,1024]{0,1:T(8,128)S(1)} %copy-done.11, f32[1024,64,64]{2,1,0:T(8,128)} %fusion.83, pred[64,64]{0,1:T(8,128)(4,1)S(1)} %iota_compare_fusion, f32[16,1024]{0,1:T(8,128)S(1)} %copy-done.12), kind=kOutput, calls=%fused_computation.20 | convolution fusion | flops 813678592 | bytes 16977920 | tf_op jit(solution)/shard_map/bjc,mbc->mjc/dot_general | solution.py:68
  435.0 1.3 copy.132
  436.3 1.5 pad_maximum_fusion.1
  437.8 1.9 collective-permute-start.1
  439.7 1.5 multiply_reduce_fusion.1
  441.3 54.7 %reduce-scatter.2.cloned.1.call-done = f32[64,4096]{1,0:T(8,128)} async-done(((f32[1024,4096]{1,0:T(8,128)}), f32[64,4096]{1,0:T(8,128)}) %reduce-scatter.2.cloned.1.call-update) | async-done | bytes 1048592 | tf_op jit(solution)/shard_map/reduce_scatter | solution.py:151
  496.0 2.1 convert_element_type.27
  498.1 7.8 %fusion.58 = f32[16,1024]{0,1:T(8,128)} fusion(f32[1024,16,2]{1,2,0:T(2,128)} %fusion.21, f32[16,1024]{0,1:T(8,128)} %copy.125, f32[2]{0:T(128)S(1)} %iota_subtract_fusion.1, f32[16,1024]{0,1:T(8,128)S(1)} %copy-done.13, f32[1,16,1024]{1,0,2:T(1,128)} %get-tuple-element.356), kind=kLoop, calls=%fused_computation.76 | loop fusion | flops 147456 | bytes 393224 | tf_op jit(solution)/shard_map/reduce_sum | solution.py:132
  510.4 1.3 fusion.42
  512.6 14.9 %all-reduce.6.cloned.1.call-done = bf16[64,4096]{1,0:T(8,128)(2,1)} async-done(((bf16[64,4096]{1,0:T(8,128)(2,1)}), bf16[64,4096]{1,0:T(8,128)(2,1)}) %all-reduce.6.cloned.1.call-update) | async-done | bytes 524304 | tf_op jit(solution)/shard_map/psum | solution.py:159
  527.5 2.1 convert_element_type.28
  529.6 130.9 %all-reduce.8.cloned.1.call-done = (f32[3,1024,7]{1,2,0:T(8,128)}, f32[1024,16]{0,1:T(8,128)}) async-done(((f32[3,1024,7]{1,2,0:T(8,128)}, f32[1024,16]{0,1:T(8,128)}), (f32[3,1024,7]{1,2,0:T(8,128)}, f32[1024,16]{0,1:T(8,128)})) %all-reduce.8.cloned.1.call-update) | async-done | bytes 151568 | tf_op jit(solution)/shard_map/psum | solution.py:148
  660.5 1.5 copy.195
  662.1 1.5 copy.196
  (170 shorter events, 50.2 us)
Async XLA Ops:
  7.2 179.6 %copy-start = (bf16[1,128,4096]{2,1,0:T(8,128)(2,1)S(1)}, bf16[1,128,4096]{2,1,0:T(8,128)(2,1)}, u32[]{:S(2)}) copy-start(bf16[1,128,4096]{2,1,0:T(8,128)(2,1)} %param.15) | copy-start | bytes 3145732
  7.2 5.0 copy-start.14
  7.2 5.0 copy-start.31
  7.2 5.8 copy-start.30
  7.2 146.7 %all-gather.12.cloned.1.call-start = ((), (), s32[]{:S(2)}) async-start(), calls=%async_computation.6 | async-start | bytes 1114112 | tf_op jit(solution)/shard_map/all_gather | solution.py:19
  10.3 6.3 collective-permute-start
  12.9 141.0 %all-gather.8.cloned.1.call-start = ((), (), s32[]{:S(2)}) async-start(), calls=%async_computation.2 | async-start | bytes 1114112 | tf_op jit(solution)/shard_map/all_gather | solution.py:19
  13.1 5.0 copy-start.16
  13.1 5.0 copy-start.18
  13.1 5.0 copy-start.20
  13.1 5.0 copy-start.22
  13.2 5.0 copy-start.24
  13.2 5.0 copy-start.26
  13.2 26.2 %copy-start.32 = (f32[2,2]{1,0:T(2,128)}, f32[2,2]{1,0:T(2,128)S(1)}, u32[]{:S(2)}) copy-start(f32[2,2]{1,0:T(2,128)S(1)} %fusion.73) | copy-start | bytes 52
  13.2 26.2 %copy-start.34 = (pred[2,2]{1,0:T(4,128)(4,1)}, pred[2,2]{1,0:T(4,128)(4,1)S(1)}, u32[]{:S(2)}) copy-start(pred[2,2]{1,0:T(4,128)(4,1)S(1)} %fusion.74) | copy-start | bytes 16
  13.3 4.9 copy-start.28
  13.5 156.4 %copy-start.10 = (f32[16,1024]{0,1:T(8,128)}, f32[16,1024]{0,1:T(8,128)S(1)}, u32[]{:S(2)}) copy-start(f32[16,1024]{0,1:T(8,128)S(1)} %copy.110) | copy-start | bytes 196612
  16.8 1.4 copy-start.1
  47.0 139.8 %all-gather.6.cloned.1.call-start = ((), (), s32[]{:S(2)}) async-start(), calls=%async_computation.1 | async-start | bytes 8912896 | tf_op jit(solution)/shard_map/all_gather | solution.py:93
  47.7 229.6 %all-gather.10.cloned.1.call-start = ((), (), s32[]{:S(2)}) async-start(), calls=%async_computation.3 | async-start | bytes 1114112 | tf_op jit(solution)/shard_map/all_gather | solution.py:19
  196.2 17.6 %copy-start.33 = (f32[2,2]{1,0:T(2,128)S(1)}, f32[2,2]{1,0:T(2,128)}, u32[]{:S(2)}) copy-start(f32[2,2]{1,0:T(2,128)} %copy-done.32) | copy-start | bytes 52
  196.2 17.6 %copy-start.35 = (pred[2,2]{1,0:T(4,128)(4,1)S(1)}, pred[2,2]{1,0:T(4,128)(4,1)}, u32[]{:S(2)}) copy-start(pred[2,2]{1,0:T(4,128)(4,1)} %copy-done.34) | copy-start | bytes 16
  220.4 275.5 %reduce-scatter.2.cloned.1.call-start = ((), (), s32[]{:S(2)}) async-start(), calls=%async_computation.4 | async-start | bytes 17825792 | tf_op jit(solution)/shard_map/reduce_scatter | solution.py:151
  319.0 0.8 copy-start.15
  319.0 1.8 copy-start.3
  319.0 1.9 copy-start.4
  319.1 208.5 %all-reduce.6.cloned.1.call-start = ((), (), s32[]{:S(2)}) async-start(), calls=%async_computation.5 | async-start | bytes 1048576 | tf_op jit(solution)/shard_map/psum | solution.py:159
  320.9 56.7 %copy-start.11 = (f32[16,1024]{0,1:T(8,128)S(1)}, f32[16,1024]{0,1:T(8,128)}, u32[]{:S(2)}) copy-start(f32[16,1024]{0,1:T(8,128)} %copy-done.10) | copy-start | bytes 196612
  320.9 56.7 %copy-start.12 = (f32[16,1024]{0,1:T(8,128)S(1)}, f32[16,1024]{0,1:T(8,128)}, u32[]{:S(2)}) copy-start(f32[16,1024]{0,1:T(8,128)} %copy.127) | copy-start | bytes 196612
  377.6 58.7 %copy-start.5 = (f32[128,1024]{1,0:T(8,128)S(1)}, f32[128,1024]{1,0:T(8,128)}, u32[]{:S(2)}) copy-start(f32[128,1024]{1,0:T(8,128)} %get-tuple-element.360) | copy-start | bytes 1572868
  434.9 4.8 copy-start.2
  436.3 3.4 copy-start.6
  436.3 3.4 copy-start.8
  437.8 70.9 %collective-permute-start.1 = (bf16[3,6,1024]{2,1,0:T(8,128)(2,1)S(1)}, bf16[3,6,1024]{2,1,0:T(8,128)(2,1)}, u32[]{:S(2)}, u32[]{:S(2)}) collective-permute-start(bf16[3,6,1024]{2,1,0:T(8,128)(2,1)S(1)} %slice.223), channel_id=1, source_target_pairs={{2,0},{4,2},{6,4},{8,6},{10,8},{12,10},{14,12},{16,14},{18,16},{20... | collective-permute-start | bytes 110600 | tf_op jit(solution)/shard_map/ppermute | solution.py:14
  441.3 56.9 %copy-start.13 = (f32[16,1024]{0,1:T(8,128)S(1)}, f32[16,1024]{0,1:T(8,128)}, u32[]{:S(2)}) copy-start(f32[16,1024]{0,1:T(8,128)} %copy.117) | copy-start | bytes 196612
  498.1 11.5 %copy-start.7 = (f32[1,128,1024]{2,1,0:T(8,128)S(1)}, f32[1,128,1024]{2,1,0:T(8,128)}, u32[]{:S(2)}) copy-start(f32[1,128,1024]{2,1,0:T(8,128)} %get-tuple-element.350) | copy-start | bytes 1572868
  498.1 11.5 %copy-start.9 = (f32[1,128,1024]{2,1,0:T(8,128)S(1)}, f32[1,128,1024]{2,1,0:T(8,128)}, u32[]{:S(2)}) copy-start(f32[1,128,1024]{2,1,0:T(8,128)} %get-tuple-element.351) | copy-start | bytes 1572868
  498.1 162.5 %all-reduce.8.cloned.1.call-start = ((), (), s32[]{:S(2)}) async-start(), calls=%async_computation.7 | async-start | bytes 327680 | tf_op jit(solution)/shard_map/psum | solution.py:148
  509.6 0.7 copy-start.17
  509.6 0.7 copy-start.19
  509.6 0.7 copy-start.21
  509.6 0.7 copy-start.23
  509.6 0.7 copy-start.25
  509.6 0.8 copy-start.27
  509.6 0.8 copy-start.29
Sparse Core Ops, SparseCore 0:
  13.1 38.3 all-gather.11
  54.1 36.8 all-gather.7
  93.2 74.0 all-gather.5
  220.5 37.2 all-gather.9
  319.2 176.7 reduce-scatter.1
  498.7 28.7 all-reduce.5
  533.7 126.8 all-reduce.7
where the time goes:
time: 682 us; the launch traced here: 671 us
  matrix products  276 us (40%)
  waiting for transfers between devices  204 us (30%)
  local copies, waits for them, and re-layouts  97.8 us (14%)
  other arithmetic  72.5 us (11%)
  between operations  15.1 us (2%)
    psum x1, waiting for transfers between devices, shards(): lax.psum((taps_part, residue_part), ('ctx', 'dp'))  131 us
    dot_general x1, matrix products, local_modes(): partial_y = jnp.einsum('bjc,mbc->mjc', correlation, growth, precision=HIGH)  57.4 us
    dot_general x1, matrix products, local_modes(): jnp.einsum('jbc,njc->nbc', toeplitz, grad_blocks, precision=HIGH)  56.8 us
    dot_general x1, matrix products, local_modes(): jnp.einsum('nbc,njc->bjc', mixed_blocks, grad_blocks, precision=HIGH)  56.6 us
    reduce_scatter x1, waiting for transfers between devices, shards(): lax.psum_scatter(lax.dot_general(gated, out_rows, (((0,), (0,)), ((), ())...  54.7 us
    gather x2, local copies, waits for them, and re-layouts, local_modes(): toeplitz = jnp.where(lower_mask[:, :, None], kernel[lag_index], 0.0)  49.5 us
    dot_general x1, matrix products, local_modes(): jnp.einsum('bjc,njc->nbc', toeplitz, mixed_blocks, precision=HIGH)  31 us
    select_n x32, other arithmetic, hop(): return jax.tree.map(lambda a, b: jnp.where(reached, a, b), new, before)  29.3 us
  transfers between devices with their start and end apart: 9, of which 4 were waited for; matrix products, arithmetic and copies ran while one was open for 54% of the time, Pallas kernels for 0%

commit v1 on v0

v1 whole, which is shorter than its diff:
```python
import functools
import math

import jax
import jax.numpy as jnp
from jax import lax
from jax.experimental import pallas as pl
from jax.experimental.pallas import tpu as pltpu
from jax.sharding import PartitionSpec as P

LANES = 128
CHUNKS = 8
HALO = 8


def at_device(ctx, dp=None):
    return {"ctx": ctx} if dp is None else {"ctx": ctx, "dp": dp}


def greet_all(ctx_count, dp_count):
    barrier = pltpu.get_barrier_semaphore()
    me, row = lax.axis_index("ctx"), lax.axis_index("dp")
    for step in range(ctx_count):
        for other in range(dp_count):
            if step + other > 0:
                pl.semaphore_signal(
                    barrier,
                    inc=1,
                    device_id=at_device(
                        lax.rem(me + step, ctx_count),
                        None if dp_count == 1 else lax.rem(row + other, dp_count),
                    ),
                    device_id_type=pl.DeviceIdType.MESH,
                )
    pl.semaphore_wait(barrier, ctx_count * dp_count - 1)


def remote(src, dst, send, recv, ctx, dp=None):
    return pltpu.make_async_remote_copy(
        src_ref=src,
        dst_ref=dst,
        send_sem=send,
        recv_sem=recv,
        device_id=at_device(ctx, dp),
        device_id_type=pl.DeviceIdType.MESH,
    )


def gather_kernel(
    group, count, x_ref, go_ref, w_ref, xg_ref, gog_ref, wg_ref, halo_ref,
    xs, xr, gs, gr, ws, wr, hs, hr, own,
):
    me = lax.axis_index("ctx")
    mine, block = lax.rem(me, group), lax.div(me, group)
    tokens = go_ref.shape[0]
    greet_all(group * count, 1)
    sends = []
    for step in range(1, count):
        there = lax.rem(block + step, count)
        sends.append(
            remote(w_ref, wg_ref.at[block], ws.at[step], wr.at[step], there * group + mine)
        )
    for step in range(1, group):
        there = lax.rem(mine + step, group)
        to = block * group + there
        sends.append(remote(x_ref.at[there], xg_ref.at[mine], xs.at[step], xr.at[step], to))
        sends.append(remote(go_ref, gog_ref.at[mine], gs.at[step], gr.at[step], to))
    for copy in sends:
        copy.start()

    def halo_copy(there):
        ahead = jnp.minimum(block + 1, count - 1)
        return remote(
            x_ref.at[there, :, pl.ds(tokens - 16, 16), :],
            halo_ref,
            hs.at[there],
            hr.at[0],
            ahead * group + there,
        )

    @pl.when((mine == group - 1) & (block < count - 1))
    def _():
        for there in range(group):
            halo_copy(there).start()

    locals_ = [
        pltpu.make_async_copy(x_ref.at[mine], xg_ref.at[mine], own.at[0]),
        pltpu.make_async_copy(go_ref, gog_ref.at[mine], own.at[1]),
        pltpu.make_async_copy(w_ref, wg_ref.at[block], own.at[2]),
    ]
    for copy in locals_:
        copy.start()
    for copy in locals_:
        copy.wait()

    @pl.when(block == 0)
    def _():
        halo_ref[...] = jnp.zeros_like(halo_ref)

    for copy in sends:
        copy.wait()

    @pl.when((mine == group - 1) & (block < count - 1))
    def _():
        for there in range(group):
            halo_copy(there).wait_send()

    @pl.when(block > 0)
    def _():
        halo_copy(0).wait_recv()


def tree_sum(parts):
    parts = list(parts)
    while len(parts) > 1:
        parts = [
            parts[k] + parts[k + 1] if k + 1 < len(parts) else parts[k]
            for k in range(0, len(parts), 2)
        ]
    return parts[0]


def scan_kernel(
    group, count, x_ref, up_ref, taps_ref, factor_ref, coef_ref, chunk_ref, whole_ref,
    fore_ref, back_ref, norm_ref, y_ref, gated_ref, small_ref,
    shaped, mixed, gradf, gext, starts, bstarts, states, hsend, hrecv,
    ss, sr, hss, hsr,
):
    me = lax.axis_index("ctx")
    mine, block = lax.rem(me, group), lax.div(me, group)
    steps = up_ref.shape[0]
    width = up_ref.shape[2]
    modes = factor_ref.shape[0]
    greet_all(group * count, 1)
    row = lax.broadcasted_iota(jnp.int32, (CHUNKS, LANES), 0)
    spans = [slice(k, k + LANES) for k in range(0, width, LANES)]

    def down(v):
        return jnp.where(row > 0, pltpu.roll(v, 1, 0), 0.0)

    def up(v):
        return jnp.where(row < CHUNKS - 1, pltpu.roll(v, CHUNKS - 1, 0), 0.0)

    zeros = tuple(jnp.zeros((CHUNKS, LANES), jnp.float32) for _ in range(modes))
    for span in spans:

        def first(s, state):
            made = []
            for i in range(3):
                total = tree_sum(
                    [taps_ref[i, j, :, span] * x_ref[i, s + HALO - j, :, span] for j in range(7)]
                )
                shaped[i, s, :, span] = total
                made.append(total)
            value = made[1] * made[2]
            mixed[s, :, span] = value
            gradf[s, :, span] = up_ref[s, :, span] * made[0]
            return tuple(factor_ref[m, :, span] * state[m] + value for m in range(modes))

        ends = lax.fori_loop(0, steps, first, zeros)

        def first_back(k, state):
            value = gradf[steps - 1 - k, :, span]
            return tuple(factor_ref[m, :, span] * state[m] + value for m in range(modes))

        firsts = lax.fori_loop(0, steps, first_back, zeros)
        for m in range(modes):
            fs = chunk_ref[m, :, span]
            a = jnp.zeros((CHUNKS, LANES), jnp.float32)
            b = a
            for _ in range(CHUNKS - 1):
                a = down(fs * a + ends[m])
                b = up(fs * b + firsts[m])
            starts[m, :, span] = a
            bstarts[m, :, span] = b
            states[block, 0, m : m + 1, span] = (fs * a + ends[m])[CHUNKS - 1 :]
            states[block, 1, m : m + 1, span] = (fs * b + firsts[m])[:1]

    copies = [
        remote(
            states.at[block],
            states.at[block],
            ss.at[step],
            sr.at[step],
            lax.rem(block + step, count) * group + mine,
        )
        for step in range(1, count)
    ]
    for copy in copies:
        copy.start()
    for copy in copies:
        copy.wait()
    incoming = jnp.zeros((modes, width), jnp.float32)
    outgoing = incoming
    decay = whole_ref[...]
    for k in range(count):
        incoming = jnp.where(k < block, decay * incoming + states[k, 0], incoming)
        r = count - 1 - k
        outgoing = jnp.where(r > block, decay * outgoing + states[r, 1], outgoing)
    for span in spans:
        for m in range(modes):
            starts[m, :, span] += fore_ref[m, :, span] * incoming[m : m + 1, span]
            bstarts[m, :, span] += back_ref[m, :, span] * outgoing[m : m + 1, span]

    for span in spans:

        def second(s, state):
            value = mixed[s, :, span]
            new = tuple(factor_ref[m, :, span] * state[m] + value for m in range(modes))
            filtered = tree_sum([coef_ref[m, :, span] * new[m] for m in range(modes)])
            gated_ref[s, :, span] = shaped[0, s, :, span] * filtered
            gext[0, s, :, span] = up_ref[s, :, span] * filtered
            return new

        lax.fori_loop(0, steps, second, tuple(starts[m, :, span] for m in range(modes)))

        def second_back(k, carry):
            state, total = carry
            s = steps - 1 - k
            value = gradf[s, :, span]
            other = mixed[s, :, span]
            new = tuple(factor_ref[m, :, span] * state[m] + value for m in range(modes))
            total = tuple(total[m] + other * new[m] for m in range(modes))
            grad = tree_sum([coef_ref[m, :, span] * new[m] for m in range(modes)])
            gext[1, s, :, span] = grad * shaped[2, s, :, span]
            gext[2, s, :, span] = grad * shaped[1, s, :, span]
            return new, total

        _, total = lax.fori_loop(
            0, steps, second_back, (tuple(bstarts[m, :, span] for m in range(modes)), zeros)
        )
        for m in range(modes):
            small_ref[21 + m : 22 + m, span] = norm_ref[m : m + 1, span] * jnp.sum(
                total[m], axis=0, keepdims=True
            )
    small_ref[21 + modes :, :] = jnp.zeros((small_ref.shape[0] - 21 - modes, width), jnp.float32)

    for i in range(3):
        for s in range(HALO):
            hsend[i, s : s + 1, :] = gext[i, s, 0:1, :]
    ahead = remote(
        hsend, hrecv, hss.at[0], hsr.at[0], jnp.maximum(block - 1, 0) * group + mine
    )

    @pl.when(block > 0)
    def _():
        ahead.start()

    for span in spans:
        for i in range(3):

            def tap(s, sums):
                value = gext[i, s, :, span]
                return tuple(
                    sums[j] + value * x_ref[i, s + HALO - j, :, span] for j in range(7)
                )

            sums = lax.fori_loop(0, steps, tap, zeros[:7], unroll=2)
            for j in range(7):
                at = i * 7 + j
                small_ref[at : at + 1, span] = jnp.sum(sums[j], axis=0, keepdims=True)

    @pl.when(block == count - 1)
    def _():
        hrecv[...] = jnp.zeros_like(hrecv)

    @pl.when(block > 0)
    def _():
        ahead.wait_send()

    @pl.when(block < count - 1)
    def _():
        ahead.wait_recv()

    for span in spans:
        for i in range(3):
            for s in range(HALO):
                gext[i, steps + s, :, span] = jnp.where(
                    row < CHUNKS - 1,
                    pltpu.roll(gext[i, s, :, span], CHUNKS - 1, 0),
                    hrecv[i, s : s + 1, span],
                )

            def out(s, nothing):
                y_ref[i, s, :, span] = tree_sum(
                    [taps_ref[i, j, :, span] * gext[i, s + j, :, span] for j in range(7)]
                )
                return nothing

            lax.fori_loop(0, steps, out, 0, unroll=2)


def exchange_kernel(
    group, count, rows_dp, wp_ref, y_ref, small_ref, wg_ref, yo_ref, so_ref,
    wbuf, pair, sbuf, wsend, wrecv, ysend, yrecv, ssend, srecv, tsend, trecv, psend, precv, own,
):
    me, row = lax.axis_index("ctx"), lax.axis_index("dp")
    mine, block = lax.rem(me, group), lax.div(me, group)
    greet_all(group * count, rows_dp)
    weights, outs, smalls, totals, pairs = [], [], [], [], []
    members = count * rows_dp
    slot = block * rows_dp + row
    for step in range(1, members):
        there = lax.rem(slot + step, members)
        smalls.append(
            remote(
                small_ref,
                sbuf.at[slot],
                ssend.at[step],
                srecv.at[step],
                lax.div(there, rows_dp) * group + mine,
                lax.rem(there, rows_dp),
            )
        )
    for step in range(1, count):
        there = lax.rem(block + step, count)
        weights.append(
            remote(
                wp_ref.at[there], wbuf.at[step], wsend.at[step], wrecv.at[step],
                there * group + mine,
            )
        )
    for step in range(1, group):
        there = lax.rem(mine + step, group)
        to = block * group + there
        outs.append(
            remote(y_ref.at[there], yo_ref.at[mine], ysend.at[step], yrecv.at[step], to)
        )
        totals.append(
            remote(so_ref.at[mine], so_ref.at[mine], tsend.at[step], trecv.at[step], to)
        )
    for copy in smalls + weights + outs:
        copy.start()
    keep = pltpu.make_async_copy(y_ref.at[mine], yo_ref.at[mine], own.at[0])
    keep.start()
    sbuf[slot] = small_ref[...]
    for copy in smalls:
        copy.wait()
    total = sbuf[0]
    for k in range(1, members):
        total = total + sbuf[k]
    so_ref[mine] = total
    for copy in totals:
        copy.start()
    for copy in weights:
        copy.wait()
    columns = wg_ref.shape[1]
    tile = math.gcd(columns, 512)

    def add(k, nothing):
        at = pl.ds(pl.multiple_of(k * tile, tile), tile)
        value = wp_ref[block, :, at].astype(jnp.float32)
        for step in range(1, count):
            value = value + wbuf[step, :, at].astype(jnp.float32)
        pair[row, :, at] = value.astype(pair.dtype)
        return nothing

    lax.fori_loop(0, columns // tile, add, 0)
    for step in range(1, rows_dp):
        pairs.append(
            remote(
                pair.at[row], pair.at[row], psend.at[step], precv.at[step],
                me, lax.rem(row + step, rows_dp),
            )
        )
    for copy in pairs:
        copy.start()
    for copy in pairs:
        copy.wait()

    def finish(k, nothing):
        at = pl.ds(pl.multiple_of(k * tile, tile), tile)
        value = pair[0, :, at].astype(jnp.float32)
        for other in range(1, rows_dp):
            value = value + pair[other, :, at].astype(jnp.float32)
        wg_ref[:, at] = value
        return nothing

    lax.fori_loop(0, columns // tile, finish, 0)
    keep.wait()
    for copy in outs + totals:
        copy.wait()


VMEM = pl.BlockSpec(memory_space=pltpu.VMEM)
DMA = pltpu.SemaphoreType.DMA


def params(number):
    return pltpu.CompilerParams(
        collective_id=number, has_side_effects=True, vmem_limit_bytes=56 * 1024 * 1024
    )


def shards(
    query_proj, key_proj, value_proj, grad_out, out_weight, short_taps, residues, decay_rate
):
    devices, rows_dp = lax.axis_size("ctx"), lax.axis_size("dp")
    group = math.gcd(devices, 4)
    count = devices // group
    mine = lax.rem(lax.axis_index("ctx"), group)
    tokens, channels = query_proj.shape[1:]
    own_rows, columns = out_weight.shape
    width = count * own_rows
    modes = residues.shape[1]
    span_tokens = group * tokens
    steps = span_tokens // CHUNKS
    f32, bf16 = jnp.float32, jnp.bfloat16

    def parted(v):
        v = v.reshape(v.shape[:-1] + (count, group, own_rows))
        return jnp.moveaxis(v, -2, 0).reshape((group,) + v.shape[:-3] + (width,))

    def picked(v):
        return lax.dynamic_index_in_dim(parted(v), mine, 0, keepdims=False)

    streams = parted(jnp.stack([query_proj[0], key_proj[0], value_proj[0]]))
    xg, gog, wg, halo = pl.pallas_call(
        functools.partial(gather_kernel, group, count),
        out_shape=(
            jax.ShapeDtypeStruct((group, 3, tokens, width), bf16),
            jax.ShapeDtypeStruct((group, tokens, columns), bf16),
            jax.ShapeDtypeStruct((count, own_rows, columns), bf16),
            jax.ShapeDtypeStruct((3, 16, width), bf16),
        ),
        in_specs=[VMEM] * 3,
        out_specs=(VMEM,) * 4,
        scratch_shapes=[
            DMA((group,)), DMA((group,)), DMA((group,)), DMA((group,)),
            DMA((count,)), DMA((count,)), DMA((group,)), DMA((1,)), DMA((3,)),
        ],
        compiler_params=params(0),
        name="gather",
    )(streams, grad_out[0], out_weight)

    out_rows = gog.reshape(span_tokens, columns)
    upstream = lax.dot_general(
        out_rows,
        wg.reshape(width, columns),
        (((1,), (1,)), ((), ())),
        preferred_element_type=f32,
    )
    upstream = jnp.swapaxes(upstream.reshape(CHUNKS, steps, width), 0, 1)
    whole = jnp.swapaxes(xg, 0, 1).reshape(3, CHUNKS, steps, width)
    before = jnp.concatenate(
        [halo[:, None, 16 - HALO :], whole[:, :-1, steps - HALO :]], axis=1
    )
    extended = jnp.swapaxes(jnp.concatenate([before, whole], axis=2), 1, 2).astype(f32)

    taps = picked(jnp.swapaxes(short_taps, 1, 2))
    rate = picked(decay_rate.T)
    norm = jnp.sqrt(-jnp.expm1(-2.0 * rate))
    coef = picked(residues.T) * norm
    places = jnp.arange(CHUNKS, dtype=f32)[None, :, None]

    def spread(v):
        return jnp.broadcast_to(v[..., None, :], v.shape[:-1] + (CHUNKS, width))

    rate_chunk = rate[:, None, :] * steps
    y, gated, small = pl.pallas_call(
        functools.partial(scan_kernel, group, count),
        out_shape=(
            jax.ShapeDtypeStruct((3, steps, CHUNKS, width), f32),
            jax.ShapeDtypeStruct((steps, CHUNKS, width), f32),
            jax.ShapeDtypeStruct(((21 + modes + 7) // 8 * 8 + 8, width), f32),
        ),
        in_specs=[VMEM] * 10,
        out_specs=(VMEM,) * 3,
        scratch_shapes=[
            pltpu.VMEM((3, steps, CHUNKS, width), f32),
            pltpu.VMEM((steps, CHUNKS, width), f32),
            pltpu.VMEM((steps, CHUNKS, width), f32),
            pltpu.VMEM((3, steps + HALO, CHUNKS, width), f32),
            pltpu.VMEM((modes, CHUNKS, width), f32),
            pltpu.VMEM((modes, CHUNKS, width), f32),
            pltpu.VMEM((count, 2, modes, width), f32),
            pltpu.VMEM((3, HALO, width), f32),
            pltpu.VMEM((3, HALO, width), f32),
            DMA((count,)), DMA((count,)), DMA((1,)), DMA((1,)),
        ],
        compiler_params=params(1),
        name="scan",
    )(
        extended,
        upstream,
        spread(taps),
        spread(jnp.exp(-rate)),
        spread(coef),
        spread(jnp.exp(-rate * steps)),
        jnp.exp(-rate * span_tokens),
        jnp.exp(-rate_chunk * places),
        jnp.exp(-rate_chunk * (CHUNKS - 1.0 - places)),
        norm,
    )

    gated = jnp.swapaxes(gated, 0, 1).reshape(span_tokens, width).astype(bf16)
    partial = lax.dot_general(
        gated, out_rows, (((0,), (0,)), ((), ())), preferred_element_type=f32
    ).astype(bf16)
    y = jnp.swapaxes(y.astype(bf16), 1, 2).reshape(3, group, tokens, width)
    weight_grad, yo, so = pl.pallas_call(
        functools.partial(exchange_kernel, group, count, rows_dp),
        out_shape=(
            jax.ShapeDtypeStruct((own_rows, columns), f32),
            jax.ShapeDtypeStruct((group, 3, tokens, width), bf16),
            jax.ShapeDtypeStruct((group,) + small.shape, f32),
        ),
        in_specs=[VMEM] * 3,
        out_specs=(VMEM,) * 3,
        scratch_shapes=[
            pltpu.VMEM((count, own_rows, columns), bf16),
            pltpu.VMEM((rows_dp, own_rows, columns), bf16),
            pltpu.VMEM((count * rows_dp,) + small.shape, f32),
            DMA((count,)), DMA((count,)), DMA((group,)), DMA((group,)),
            DMA((count * rows_dp,)), DMA((count * rows_dp,)),
            DMA((group,)), DMA((group,)), DMA((rows_dp,)), DMA((rows_dp,)), DMA((1,)),
        ],
        compiler_params=params(2),
        name="exchange",
    )(partial.reshape(count, own_rows, columns), jnp.swapaxes(y, 0, 1), small)

    def joined(v):
        v = v.reshape(v.shape[:-1] + (count, own_rows))
        v = jnp.moveaxis(v, 0, -2)
        return v.reshape(v.shape[:-3] + (channels,))

    grads = joined(yo)
    sums = joined(so)
    taps_grad = jnp.swapaxes(sums[:21].reshape(3, 7, channels), 1, 2)
    residue_grad = sums[21 : 21 + modes].T
    return (grads[0][None], grads[1][None], grads[2][None], weight_grad, taps_grad, residue_grad)


def solution(mesh):
    placed = (
        P("dp", "ctx", None),
        P("dp", "ctx", None),
        P("dp", "ctx", None),
        P("dp", "ctx", None),
        P("ctx", None),
        P(),
        P(),
        P(),
    )
    return jax.shard_map(
        shards,
        mesh=mesh,
        in_specs=placed,
        out_specs=(
            P("dp", "ctx", None),
            P("dp", "ctx", None),
            P("dp", "ctx", None),
            P("ctx", None),
            P(),
            P(),
        ),
        check_vma=False,
    )
```

time: 682 us -> 193 us (0.28); the launches traced: 671 us -> 193 us
  matrix products: 276 us -> 6.07 us
  waiting for transfers between devices: 204 us -> 0 us
  Pallas kernels: 0 us -> 162 us
  local copies, waits for them, and re-layouts: 97.8 us -> 19.8 us
  other arithmetic: 72.5 us -> 4.08 us
  between operations: 15.1 us -> 0.95 us
    dot_general x9 -> x1, matrix products: 268 us -> 3.47 us  [shards(): lax.dot_general(out_rows, wg.reshape(width, columns), (((1,), (1,)), ((),...]
    pallas_call x0 -> x3, Pallas kernels: none -> 162 us  [the longest x1 74.3 us: shards(): pl.pallas_call(functools.partial(exchange_kernel, group, count, rows_dp),...]
    psum x2 -> x0, waiting for transfers between devices: 146 us -> none  [the longest x1 131 us: shards(): lax.psum((taps_part, residue_part), ('ctx', 'dp'))]
    reduce_scatter x1 -> x0, waiting for transfers between devices: 54.7 us -> none  [shards(): lax.psum_scatter(lax.dot_general(gated, out_rows, (((0,), (0,)), ((), ())...]
    gather x2 -> x0, local copies, waits for them, and re-layouts: 49.5 us -> none  [local_modes(): toeplitz = jnp.where(lower_mask[:, :, None], kernel[lag_index], 0.0)]
    select_n x32 -> x0, other arithmetic: 29.3 us -> none  [hop(): return jax.tree.map(lambda a, b: jnp.where(reached, a, b), new, before)]
    unnamed x5 -> x0, other arithmetic: 17.4 us -> none
    slice x8 -> x10, local copies, waits for them, and re-layouts: 11.4 us -> 1.06 us  [the longest x3 0.88 us: shards(): residue_grad = sums[21:21 + modes].T]
  transfers between devices with their start and end apart: 9 -> 0, of which waited for: 4 -> 0; matrix products, arithmetic and copies ran while one was open for 54% -> 0% of each run, Pallas kernels for 0% -> 0%
where the time goes in v1:
time: 193 us
  Pallas kernels  162 us (84%)
  local copies, waits for them, and re-layouts  19.8 us (10%)
  matrix products  6.07 us (3%)
  other arithmetic  4.08 us (2%)
    pallas_call x1, Pallas kernels, shards(): pl.pallas_call(functools.partial(exchange_kernel, group, count, rows_dp),...  74.3 us
    pallas_call x1, Pallas kernels, shards(): pl.pallas_call(functools.partial(gather_kernel, group, count), out_shape=...  62.2 us
    pallas_call x1, Pallas kernels, shards(): pl.pallas_call(functools.partial(scan_kernel, group, count), out_shape=(j...  25.6 us
    unnamed x24, local copies, waits for them, and re-layouts  4.06 us

profile of v1, /device:TPU:8, one launch (start us, length us, event | category | flops | bytes accessed | tf_op | source)
XLA Modules:
  0.0 193.0 jit_solution(16190869235953999564)
XLA Ops:
  0.6 0.0 copy-start.4
  0.6 0.0 copy-start.3
  0.7 1.0 reshape.138
  1.7 0.1 reshape.139
  1.9 1.0 reshape.136
  2.9 0.1 reshape.137
  3.0 0.6 sqrt_bitcast_fusion
  3.7 0.7 broadcast_in_dim.16.coef_ref
  4.4 0.7 broadcast_in_dim.17.chunk_ref
  5.0 0.7 broadcast_in_dim.15.factor_ref
  5.7 1.0 reshape.134
  6.8 0.1 reshape.135
  7.0 0.7 broadcast_in_dim.14.taps_ref
  7.6 0.8 multiply_exponential_fusion
  8.4 0.0 copy-done.3
  8.4 0.2 copy.23
  8.6 0.0 copy-done.4
  8.6 0.2 copy.24
  8.8 0.0 copy-done.5
  8.8 0.2 copy.25
  8.9 0.1 pad_maximum_fusion
  9.0 0.1 copy.26
  9.1 1.2 copy.27.x_ref
  10.3 62.2 %gather.1 = (bf16[4,3,128,256]{3,2,1,0:T(8,128)(2,1)}, bf16[4,128,4096]{2,1,0:T(8,128)(2,1)}, bf16[4,64,4096]{2,1,0:T(8,128)(2,1)}, bf16[3,16,256]{2,1,0:T(8,128)(2,1)}) custom-call(bf16[4,3,128,256]{3,2,1,0:T(8,128)(2,1)} %copy.27.x_ref, bf16[128,4096]{1,0:T(8,128)(2,1)} %bitcast.86, bf16[64,4096]{1,0:T(8,128)(2,1)} %w_ref.1), custom_call_target="tpu_custom_call" | custom-call | tf_op jit(solution)/shard_map/gather/pallas_call | solution.py:418
  72.5 0.0 copy-start.7
  72.5 0.9 slice_bitcast_fusion
  73.3 1.2 copy.28
  74.5 0.4 copy.29
  75.0 3.5 %fusion.1 = f32[8,64,256]{2,1,0:T(8,128)S(1)} fusion(bf16[8,64,4096]{2,1,0:T(8,128)(2,1)} %bitcast.75, bf16[256,4096,1]{1,0,2:T(8,128)(2,1)S(1)} %bitcast.100), kind=kOutput, calls=%fused_computation.22 | convolution fusion | flops 1073741824 | bytes 6815744 | tf_op jit(solution)/shard_map/dot_general | solution.py:437
  78.5 1.1 copy.54
  79.6 1.4 convert_bitcast_fusion.x_ref
  81.0 25.6 %scan.1 = (f32[3,64,8,256]{3,2,1,0:T(8,128)}, f32[64,8,256]{2,1,0:T(8,128)}, f32[48,256]{1,0:T(8,128)}) custom-call(f32[3,72,8,256]{3,2,1,0:T(8,128)} %convert_bitcast_fusion.x_ref, f32[64,8,256]{2,1,0:T(8,128)} %bitcast.82, f32[3,7,8,256]{3,2,1,0:T(8,128)} %broadcast_in_dim.14.taps_ref, f32[16,8,256]{2,1,0:T(8,128)} %broadcast_in_dim.15.factor_ref, ...), custom_call_target="tpu_custom_call" | custom-call | tf_op jit(solution)/shard_map/scan/pallas_call | solution.py:460
  106.6 1.1 convert_bitcast_fusion.2
  107.8 2.6 %convolution_convert_fusion = bf16[256,4096]{1,0:T(8,128)(2,1)} fusion(bf16[512,256]{1,0:T(8,128)(2,1)S(1)} %bitcast.85, bf16[512,4096]{1,0:T(8,128)(2,1)S(1)} %bitcast.76), kind=kOutput, calls=%fused_computation | convolution fusion | flops 1074790400 | bytes 6553600 | tf_op jit(solution)/shard_map/dot_general | solution.py:497
  110.4 0.1 convert_bitcast_fusion.1
  110.5 0.2 copy.37
  110.6 0.9 copy_bitcast_fusion.y_ref
  111.6 74.3 %exchange.1 = (f32[64,4096]{1,0:T(8,128)}, bf16[4,3,128,256]{3,2,1,0:T(8,128)(2,1)}, f32[4,48,256]{2,1,0:T(8,128)}) custom-call(bf16[4,64,4096]{2,1,0:T(8,128)(2,1)} %bitcast.74, bf16[4,3,128,256]{3,2,1,0:T(8,128)(2,1)} %copy_bitcast_fusion.y_ref, f32[48,256]{1,0:T(8,128)} %get-tuple-element.22.small_ref), custom_call_target="tpu_custom_call" | custom-call | tf_op jit(solution)/shard_map/exchange/pallas_call | solution.py:501
  185.9 1.5 copy.39
  187.4 0.1 fusion
  187.5 0.9 copy.47
  188.4 0.9 copy.46
  189.2 0.9 copy.45
  190.1 0.2 reshape.144
  190.4 0.8 reshape.145
  191.2 0.1 copy.44
  191.3 0.8 slice.44
  192.0 1.0 copy.59
  (26 shorter events, 0.4 us)
Async XLA Ops:
  0.6 8.0 %copy-start.4 = (bf16[1,128,1024]{2,1,0:T(8,128)(2,1)S(1)}, bf16[1,128,1024]{2,1,0:T(8,128)(2,1)}, u32[]{:S(2)}) copy-start(bf16[1,128,1024]{2,1,0:T(8,128)(2,1)} %param.9) | copy-start | bytes 786436
  0.6 7.8 %copy-start.3 = (bf16[1,128,1024]{2,1,0:T(8,128)(2,1)S(1)}, bf16[1,128,1024]{2,1,0:T(8,128)(2,1)}, u32[]{:S(2)}) copy-start(bf16[1,128,1024]{2,1,0:T(8,128)(2,1)} %param.8) | copy-start | bytes 786436
  1.7 7.1 %copy-start.5 = (bf16[1,128,1024]{2,1,0:T(8,128)(2,1)S(1)}, bf16[1,128,1024]{2,1,0:T(8,128)(2,1)}, u32[]{:S(2)}) copy-start(bf16[1,128,1024]{2,1,0:T(8,128)(2,1)} %param.10) | copy-start | bytes 786436
  72.5 2.5 %copy-start.7 = (bf16[4,64,4096]{2,1,0:T(8,128)(2,1)S(1)}, bf16[4,64,4096]{2,1,0:T(8,128)(2,1)}, u32[]{:S(2)}) copy-start(bf16[4,64,4096]{2,1,0:T(8,128)(2,1)} %get-tuple-element.19) | copy-start | bytes 6291460
  81.0 26.8 %copy-start = (bf16[4,128,4096]{2,1,0:T(8,128)(2,1)S(1)}, bf16[4,128,4096]{2,1,0:T(8,128)(2,1)}, u32[]{:S(2)}) copy-start(bf16[4,128,4096]{2,1,0:T(8,128)(2,1)} %get-tuple-element.18) | copy-start | bytes 12582916
  107.8 2.6 %copy-start.1 = (f32[3,64,8,256]{3,2,1,0:T(8,128)S(1)}, f32[3,64,8,256]{3,2,1,0:T(8,128)}, u32[]{:S(2)}) copy-start(f32[3,64,8,256]{3,2,1,0:T(8,128)} %get-tuple-element.21) | copy-start | bytes 4718596
  187.4 2.7 %copy-start.6 = (f32[4,48,256]{2,1,0:T(8,128)S(1)}, f32[4,48,256]{2,1,0:T(8,128)}, u32[]{:S(2)}) copy-start(f32[4,48,256]{2,1,0:T(8,128)} %get-tuple-element.25) | copy-start | bytes 589828
  188.3 3.7 %copy-start.2 = (f32[64,4096]{1,0:T(8,128)S(1)}, f32[64,4096]{1,0:T(8,128)}, u32[]{:S(2)}) copy-start(f32[64,4096]{1,0:T(8,128)} %get-tuple-element.51) | copy-start | bytes 3145732

commit v2 on v1

--- a/solution.py
+++ b/solution.py
@@ -11,6 +11,7 @@
 LANES = 128
 CHUNKS = 8
 HALO = 8
+PIECES = 4
 
 
 def at_device(ctx, dp=None):
@@ -47,25 +48,53 @@
 
 
 def gather_kernel(
-    group, count, x_ref, go_ref, w_ref, xg_ref, gog_ref, wg_ref, halo_ref,
-    xs, xr, gs, gr, ws, wr, hs, hr, own,
+    group, count, rows_dp, x_ref, go_ref, w_ref, xg_ref, gog_ref, wg_ref, halo_ref,
+    xs, xr, gs, gr, fs, fr, ts, tr, ws, wr, ps, pr, hs, hr, own,
 ):
-    me = lax.axis_index("ctx")
+    me, row = lax.axis_index("ctx"), lax.axis_index("dp")
     mine, block = lax.rem(me, group), lax.div(me, group)
     tokens = go_ref.shape[0]
-    greet_all(group * count, 1)
-    sends = []
+    part = w_ref.shape[1] // rows_dp
+    columns = pl.ds(pl.multiple_of(row * part, part), part)
+    pieces = gs.shape[0]
+    tall = tokens // pieces
+    across = lax.rem(mine + group // 2, group)
+    twin = mine + 1 - 2 * lax.rem(mine, 2)
+    home = block * group
+    greet_all(group * count, rows_dp)
+    weights = [
+        remote(
+            w_ref.at[:, columns],
+            wg_ref.at[block, :, columns],
+            ws.at[step],
+            wr.at[step],
+            lax.rem(block + step, count) * group + mine,
+        )
+        for step in range(1, count)
+    ]
+    swaps = []
     for step in range(1, count):
-        there = lax.rem(block + step, count)
-        sends.append(
-            remote(w_ref, wg_ref.at[block], ws.at[step], wr.at[step], there * group + mine)
-        )
+        held = wg_ref.at[lax.rem(block + count - step, count), :, columns]
+        for other in range(1, rows_dp):
+            at = step * rows_dp + other
+            to = lax.rem(row + other, rows_dp)
+            swaps.append((step, remote(held, held, ps.at[at], pr.at[at], me, to)))
+    over, passed = [], []
+    for k in range(pieces):
+        tile = pl.ds(k * tall, tall)
+        over.append(
+            remote(go_ref.at[tile], gog_ref.at[mine, tile], gs.at[k], gr.at[k], home + across)
+        )
+        held = gog_ref.at[across, tile]
+        passed.append(remote(held, held, fs.at[k], fr.at[k], home + twin))
+    beside = remote(go_ref, gog_ref.at[mine], ts.at[0], tr.at[0], home + twin)
+    streams = []
     for step in range(1, group):
         there = lax.rem(mine + step, group)
-        to = block * group + there
-        sends.append(remote(x_ref.at[there], xg_ref.at[mine], xs.at[step], xr.at[step], to))
-        sends.append(remote(go_ref, gog_ref.at[mine], gs.at[step], gr.at[step], to))
-    for copy in sends:
+        streams.append(
+            remote(x_ref.at[there], xg_ref.at[mine], xs.at[step], xr.at[step], home + there)
+        )
+    for copy in weights + over + streams + [beside]:
         copy.start()
 
     def halo_copy(there):
@@ -90,14 +119,29 @@
     ]
     for copy in locals_:
         copy.start()
-    for copy in locals_:
-        copy.wait()
 
     @pl.when(block == 0)
     def _():
         halo_ref[...] = jnp.zeros_like(halo_ref)
 
-    for copy in sends:
+    def relay(k):
+        over[k].wait_recv()
+        passed[k].start()
+
+    for k in range(pieces // 2):
+        relay(k)
+    for step in range(1, count):
+        weights[step - 1].wait_recv()
+        for at, copy in swaps:
+            if at == step:
+                copy.start()
+        if pieces // 2 + step - 1 < pieces:
+            relay(pieces // 2 + step - 1)
+    for k in range(pieces // 2 + count - 1, pieces):
+        relay(k)
+    for copy in weights + over:
+        copy.wait_send()
+    for copy in locals_ + streams + passed + [beside] + [copy for _, copy in swaps]:
         copy.wait()
 
     @pl.when((mine == group - 1) & (block < count - 1))
@@ -121,8 +165,8 @@
 
 
 def scan_kernel(
-    group, count, x_ref, up_ref, taps_ref, factor_ref, coef_ref, chunk_ref, whole_ref,
-    fore_ref, back_ref, norm_ref, y_ref, gated_ref, small_ref,
+    group, count, x_ref, up_ref, taps_row, factor_row, coef_row, rate_row, norm_ref,
+    y_ref, gated_ref, small_ref, taps_ref, factor_ref, coef_ref,
     shaped, mixed, gradf, gext, starts, bstarts, states, hsend, hrecv,
     ss, sr, hss, hsr,
 ):
@@ -132,6 +176,12 @@
     width = up_ref.shape[2]
     modes = factor_ref.shape[0]
     greet_all(group * count, 1)
+    for m in range(modes):
+        factor_ref[m] = jnp.broadcast_to(factor_row[m : m + 1], (CHUNKS, width))
+        coef_ref[m] = jnp.broadcast_to(coef_row[m : m + 1], (CHUNKS, width))
+    for i in range(3):
+        for j in range(7):
+            taps_ref[i, j] = jnp.broadcast_to(taps_row[i, j : j + 1], (CHUNKS, width))
     row = lax.broadcasted_iota(jnp.int32, (CHUNKS, LANES), 0)
     spans = [slice(k, k + LANES) for k in range(0, width, LANES)]
 
@@ -165,7 +215,9 @@
 
         firsts = lax.fori_loop(0, steps, first_back, zeros)
         for m in range(modes):
-            fs = chunk_ref[m, :, span]
+            fs = jnp.broadcast_to(
+                jnp.exp(-rate_row[m : m + 1, span] * float(steps)), (CHUNKS, LANES)
+            )
             a = jnp.zeros((CHUNKS, LANES), jnp.float32)
             b = a
             for _ in range(CHUNKS - 1):
@@ -192,15 +244,18 @@
         copy.wait()
     incoming = jnp.zeros((modes, width), jnp.float32)
     outgoing = incoming
-    decay = whole_ref[...]
+    decay = jnp.exp(-rate_row[...] * float(steps * CHUNKS))
+    place = row.astype(jnp.float32) * float(steps)
     for k in range(count):
         incoming = jnp.where(k < block, decay * incoming + states[k, 0], incoming)
         r = count - 1 - k
         outgoing = jnp.where(r > block, decay * outgoing + states[r, 1], outgoing)
     for span in spans:
         for m in range(modes):
-            starts[m, :, span] += fore_ref[m, :, span] * incoming[m : m + 1, span]
-            bstarts[m, :, span] += back_ref[m, :, span] * outgoing[m : m + 1, span]
+            rate = rate_row[m : m + 1, span]
+            starts[m, :, span] += jnp.exp(-rate * place) * incoming[m : m + 1, span]
+            far = float(steps * (CHUNKS - 1)) - place
+            bstarts[m, :, span] += jnp.exp(-rate * far) * outgoing[m : m + 1, span]
 
     for span in spans:
 
@@ -292,14 +347,20 @@
 
 def exchange_kernel(
     group, count, rows_dp, wp_ref, y_ref, small_ref, wg_ref, yo_ref, so_ref,
-    wbuf, pair, sbuf, wsend, wrecv, ysend, yrecv, ssend, srecv, tsend, trecv, psend, precv, own,
+    wbuf, pair, qbuf, qsum, qz, qpair, sbuf,
+    wsend, wrecv, ysend, yrecv, ssend, srecv, tsend, trecv, psend, precv,
+    qsend, qrecv, zsend, zrecv, fsend, frecv, own,
 ):
     me, row = lax.axis_index("ctx"), lax.axis_index("dp")
     mine, block = lax.rem(me, group), lax.div(me, group)
+    f32 = jnp.float32
+    half = pair.shape[2]
+    part = qpair.shape[2]
+    tile = math.gcd(part, 512)
     greet_all(group * count, rows_dp)
-    weights, outs, smalls, totals, pairs = [], [], [], [], []
     members = count * rows_dp
     slot = block * rows_dp + row
+    smalls = []
     for step in range(1, members):
         there = lax.rem(slot + step, members)
         smalls.append(
@@ -312,14 +373,33 @@
                 lax.rem(there, rows_dp),
             )
         )
+    weights, sums = [], []
     for step in range(1, count):
         there = lax.rem(block + step, count)
+        to = there * group + mine
         weights.append(
             remote(
-                wp_ref.at[there], wbuf.at[step], wsend.at[step], wrecv.at[step],
-                there * group + mine,
+                wp_ref.at[there, :, pl.ds(0, half)], wbuf.at[step], wsend.at[step],
+                wrecv.at[step], to,
             )
         )
+        sums.append(remote(qsum.at[there], qz.at[step], zsend.at[step], zrecv.at[step], to))
+    quarters, pairs, finals = [], [], []
+    for step in range(1, rows_dp):
+        to = lax.rem(row + step, rows_dp)
+        columns = pl.ds(pl.multiple_of(half + to * part, part), part)
+        quarters.append(
+            remote(
+                wp_ref.at[:, :, columns], qbuf.at[step], qsend.at[step], qrecv.at[step], me, to
+            )
+        )
+        pairs.append(
+            remote(pair.at[row], pair.at[row], psend.at[step], precv.at[step], me, to)
+        )
+        finals.append(
+            remote(qpair.at[row], qpair.at[row], fsend.at[step], frecv.at[step], me, to)
+        )
+    outs, totals = [], []
     for step in range(1, group):
         there = lax.rem(mine + step, group)
         to = block * group + there
@@ -329,11 +409,34 @@
         totals.append(
             remote(so_ref.at[mine], so_ref.at[mine], tsend.at[step], trecv.at[step], to)
         )
-    for copy in smalls + weights + outs:
+    for copy in quarters + weights + outs + smalls:
         copy.start()
     keep = pltpu.make_async_copy(y_ref.at[mine], yo_ref.at[mine], own.at[0])
     keep.start()
     sbuf[slot] = small_ref[...]
+
+    def each(width, body):
+        def run(k, nothing):
+            body(pl.multiple_of(k * tile, tile))
+            return nothing
+
+        lax.fori_loop(0, width // tile, run, 0)
+
+    for copy in quarters:
+        copy.wait()
+
+    def add_rows(at):
+        source = pl.ds(pl.multiple_of(half + row * part + at, tile), tile)
+        at = pl.ds(at, tile)
+        for k in range(count):
+            value = wp_ref[k, :, source].astype(f32)
+            for step in range(1, rows_dp):
+                value = value + qbuf[step, k, :, at].astype(f32)
+            qsum[k, :, at] = value.astype(qsum.dtype)
+
+    each(part, add_rows)
+    for copy in sums:
+        copy.start()
     for copy in smalls:
         copy.wait()
     total = sbuf[0]
@@ -344,39 +447,50 @@
         copy.start()
     for copy in weights:
         copy.wait()
-    columns = wg_ref.shape[1]
-    tile = math.gcd(columns, 512)
-
-    def add(k, nothing):
-        at = pl.ds(pl.multiple_of(k * tile, tile), tile)
-        value = wp_ref[block, :, at].astype(jnp.float32)
+
+    def add(at):
+        at = pl.ds(at, tile)
+        value = wp_ref[block, :, at].astype(f32)
         for step in range(1, count):
-            value = value + wbuf[step, :, at].astype(jnp.float32)
+            value = value + wbuf[step, :, at].astype(f32)
         pair[row, :, at] = value.astype(pair.dtype)
-        return nothing
-
-    lax.fori_loop(0, columns // tile, add, 0)
-    for step in range(1, rows_dp):
-        pairs.append(
-            remote(
-                pair.at[row], pair.at[row], psend.at[step], precv.at[step],
-                me, lax.rem(row + step, rows_dp),
-            )
-        )
+
+    each(half, add)
     for copy in pairs:
         copy.start()
+    for copy in sums:
+        copy.wait()
+
+    def add_blocks(at):
+        at = pl.ds(at, tile)
+        value = qsum[block, :, at].astype(f32)
+        for step in range(1, count):
+            value = value + qz[step, :, at].astype(f32)
+        qpair[row, :, at] = value.astype(qpair.dtype)
+
+    each(part, add_blocks)
+    for copy in finals:
+        copy.start()
     for copy in pairs:
         copy.wait()
 
-    def finish(k, nothing):
-        at = pl.ds(pl.multiple_of(k * tile, tile), tile)
-        value = pair[0, :, at].astype(jnp.float32)
+    def finish(at):
+        at = pl.ds(at, tile)
+        value = pair[0, :, at].astype(f32)
         for other in range(1, rows_dp):
-            value = value + pair[other, :, at].astype(jnp.float32)
+            value = value + pair[other, :, at].astype(f32)
         wg_ref[:, at] = value
-        return nothing
-
-    lax.fori_loop(0, columns // tile, finish, 0)
+
+    each(half, finish)
+    for copy in finals:
+        copy.wait()
+    for other in range(rows_dp):
+
+        def finish_part(at):
+            to = pl.ds(pl.multiple_of(half + other * part + at, tile), tile)
+            wg_ref[:, to] = qpair[other, :, pl.ds(at, tile)].astype(f32)
+
+        each(part, finish_part)
     keep.wait()
     for copy in outs + totals:
         copy.wait()
@@ -406,6 +520,8 @@
     span_tokens = group * tokens
     steps = span_tokens // CHUNKS
     f32, bf16 = jnp.float32, jnp.bfloat16
+    half = columns // 2
+    part = half // rows_dp
 
     def parted(v):
         v = v.reshape(v.shape[:-1] + (count, group, own_rows))
@@ -416,7 +532,7 @@
 
     streams = parted(jnp.stack([query_proj[0], key_proj[0], value_proj[0]]))
     xg, gog, wg, halo = pl.pallas_call(
-        functools.partial(gather_kernel, group, count),
+        functools.partial(gather_kernel, group, count, rows_dp),
         out_shape=(
             jax.ShapeDtypeStruct((group, 3, tokens, width), bf16),
             jax.ShapeDtypeStruct((group, tokens, columns), bf16),
@@ -426,8 +542,10 @@
         in_specs=[VMEM] * 3,
         out_specs=(VMEM,) * 4,
         scratch_shapes=[
-            DMA((group,)), DMA((group,)), DMA((group,)), DMA((group,)),
-            DMA((count,)), DMA((count,)), DMA((group,)), DMA((1,)), DMA((3,)),
+            DMA((group,)), DMA((group,)), DMA((PIECES,)), DMA((PIECES,)),
+            DMA((PIECES,)), DMA((PIECES,)), DMA((1,)), DMA((1,)),
+            DMA((count,)), DMA((count,)), DMA((count * rows_dp,)), DMA((count * rows_dp,)),
+            DMA((group,)), DMA((1,)), DMA((3,)),
         ],
         compiler_params=params(0),
         name="gather",
@@ -451,12 +569,6 @@
     rate = picked(decay_rate.T)
     norm = jnp.sqrt(-jnp.expm1(-2.0 * rate))
     coef = picked(residues.T) * norm
-    places = jnp.arange(CHUNKS, dtype=f32)[None, :, None]
-
-    def spread(v):
-        return jnp.broadcast_to(v[..., None, :], v.shape[:-1] + (CHUNKS, width))
-
-    rate_chunk = rate[:, None, :] * steps
     y, gated, small = pl.pallas_call(
         functools.partial(scan_kernel, group, count),
         out_shape=(
@@ -464,9 +576,12 @@
             jax.ShapeDtypeStruct((steps, CHUNKS, width), f32),
             jax.ShapeDtypeStruct(((21 + modes + 7) // 8 * 8 + 8, width), f32),
         ),
-        in_specs=[VMEM] * 10,
+        in_specs=[VMEM] * 7,
         out_specs=(VMEM,) * 3,
         scratch_shapes=[
+            pltpu.VMEM((3, 7, CHUNKS, width), f32),
+            pltpu.VMEM((modes, CHUNKS, width), f32),
+            pltpu.VMEM((modes, CHUNKS, width), f32),
             pltpu.VMEM((3, steps, CHUNKS, width), f32),
             pltpu.VMEM((steps, CHUNKS, width), f32),
             pltpu.VMEM((steps, CHUNKS, width), f32),
@@ -483,13 +598,10 @@
     )(
         extended,
         upstream,
-        spread(taps),
-        spread(jnp.exp(-rate)),
-        spread(coef),
-        spread(jnp.exp(-rate * steps)),
-        jnp.exp(-rate * span_tokens),
-        jnp.exp(-rate_chunk * places),
-        jnp.exp(-rate_chunk * (CHUNKS - 1.0 - places)),
+        taps,
+        jnp.exp(-rate),
+        coef,
+        rate,
         norm,
     )
 
@@ -508,12 +620,18 @@
         in_specs=[VMEM] * 3,
         out_specs=(VMEM,) * 3,
         scratch_shapes=[
-            pltpu.VMEM((count, own_rows, columns), bf16),
-            pltpu.VMEM((rows_dp, own_rows, columns), bf16),
+            pltpu.VMEM((count, own_rows, half), bf16),
+            pltpu.VMEM((rows_dp, own_rows, half), bf16),
+            pltpu.VMEM((rows_dp, count, own_rows, part), bf16),
+            pltpu.VMEM((count, own_rows, part), bf16),
+            pltpu.VMEM((count, own_rows, part), bf16),
+            pltpu.VMEM((rows_dp, own_rows, part), bf16),
             pltpu.VMEM((count * rows_dp,) + small.shape, f32),
             DMA((count,)), DMA((count,)), DMA((group,)), DMA((group,)),
             DMA((count * rows_dp,)), DMA((count * rows_dp,)),
-            DMA((group,)), DMA((group,)), DMA((rows_dp,)), DMA((rows_dp,)), DMA((1,)),
+            DMA((group,)), DMA((group,)), DMA((rows_dp,)), DMA((rows_dp,)),
+            DMA((rows_dp,)), DMA((rows_dp,)), DMA((count,)), DMA((count,)),
+            DMA((rows_dp,)), DMA((rows_dp,)), DMA((1,)),
         ],
         compiler_params=params(2),
         name="exchange",

time: 193 us -> 156 us (0.81)
  Pallas kernels: 162 us -> 127 us
  local copies, waits for them, and re-layouts: 19.8 us -> 17.8 us
    pallas_call x1, Pallas kernels: 62.2 us -> 40.9 us  [shards(): pl.pallas_call(functools.partial(gather_kernel, group, count, rows_dp), o...]
    pallas_call x1, Pallas kernels: 74.3 us -> 55.8 us  [shards(): pl.pallas_call(functools.partial(exchange_kernel, group, count, rows_dp),...]
    pallas_call x1, Pallas kernels: 25.6 us -> 29.8 us  [shards(): pl.pallas_call(functools.partial(scan_kernel, group, count), out_shape=(j...]
    broadcast_in_dim x4 -> x0, local copies, waits for them, and re-layouts: 2.69 us -> none  [spread(): return jnp.broadcast_to(v[..., None, :], v.shape[:-1] + (CHUNKS, width))]
    unnamed x24 -> x26, local copies, waits for them, and re-layouts: 4.06 us -> 4.67 us
where the time goes in v2:
time: 156 us; the launch traced here: 155 us
  Pallas kernels  127 us (81%)
  local copies, waits for them, and re-layouts  17.8 us (11%)
  matrix products  6.09 us (4%)
  other arithmetic  3.92 us (3%)
    pallas_call x1, Pallas kernels, shards(): pl.pallas_call(functools.partial(exchange_kernel, group, count, rows_dp),...  55.8 us
    pallas_call x1, Pallas kernels, shards(): pl.pallas_call(functools.partial(gather_kernel, group, count, rows_dp), o...  40.9 us
    pallas_call x1, Pallas kernels, shards(): pl.pallas_call(functools.partial(scan_kernel, group, count), out_shape=(j...  29.8 us
    unnamed x26, local copies, waits for them, and re-layouts  4.67 us
    dot_general x1, matrix products, shards(): lax.dot_general(out_rows, wg.reshape(width, columns), (((1,), (1,)), ((),...  3.47 us

profile of v2, /device:TPU:8, one launch (start us, length us, event | category | flops | bytes accessed | tf_op | source)
XLA Modules:
  0.0 155.3 jit_solution(1273453008457018060)
XLA Ops:
  0.6 0.0 copy-start.5
  0.6 0.0 copy-start.4
  0.7 0.0 copy-start.3
  0.7 1.0 reshape.81
  1.7 0.1 reshape.82
  1.9 1.0 reshape.79
  2.9 0.1 reshape.80
  3.0 0.6 negate_sqrt_fusion
  3.6 0.6 bitcast_multiply_fusion
  4.3 1.0 reshape.77
  5.4 0.1 reshape.78
  5.5 0.6 copy.56
  6.1 0.0 copy-done.3
  6.1 0.2 copy.24
  6.3 0.0 copy-done.4
  6.3 0.2 copy.25
  6.5 0.0 copy-done.5
  6.5 0.2 copy.26
  6.7 0.1 pad_maximum_fusion
  6.8 0.1 copy.27
  6.8 0.0 copy-done.7
  6.8 1.2 copy.28.x_ref
  8.0 40.9 %gather.1 = (bf16[4,3,128,256]{3,2,1,0:T(8,128)(2,1)}, bf16[4,128,4096]{2,1,0:T(8,128)(2,1)}, bf16[4,64,4096]{2,1,0:T(8,128)(2,1)}, bf16[3,16,256]{2,1,0:T(8,128)(2,1)}) custom-call(bf16[4,3,128,256]{3,2,1,0:T(8,128)(2,1)} %copy.28.x_ref, bf16[128,4096]{1,0:T(8,128)(2,1)} %bitcast.75, bf16[64,4096]{1,0:T(8,128)(2,1)} %w_ref.1), custom_call_target="tpu_custom_call" | custom-call | tf_op jit(solution)/shard_map/gather/pallas_call | solution.py:534
  49.0 0.9 slice_bitcast_fusion
  49.8 1.2 copy.29
  51.0 0.4 copy.30
  51.5 3.5 %fusion.1 = f32[8,64,256]{2,1,0:T(8,128)S(1)} fusion(bf16[8,64,4096]{2,1,0:T(8,128)(2,1)} %bitcast.64, bf16[256,4096,1]{1,0,2:T(8,128)(2,1)S(1)} %bitcast.89), kind=kOutput, calls=%fused_computation.16 | convolution fusion | flops 1073741824 | bytes 6815744 | tf_op jit(solution)/shard_map/dot_general | solution.py:555
  55.0 1.1 copy.54
  56.1 1.4 convert_bitcast_fusion.x_ref
  57.5 29.8 %scan.1 = (f32[3,64,8,256]{3,2,1,0:T(8,128)}, f32[64,8,256]{2,1,0:T(8,128)}, f32[48,256]{1,0:T(8,128)}) custom-call(f32[3,72,8,256]{3,2,1,0:T(8,128)} %convert_bitcast_fusion.x_ref, f32[64,8,256]{2,1,0:T(8,128)} %bitcast.71, f32[3,7,256]{2,1,0:T(8,128)} %bitcast.83, f32[16,256]{1,0:T(8,128)} %get-tuple-element.38.factor_row, ...), custom_call_target="tpu_custom_call" | custom-call | tf_op jit(solution)/shard_map/scan/pallas_call | solution.py:572
  87.4 1.1 convert_bitcast_fusion.2
  88.5 2.6 %convolution_convert_fusion = bf16[256,4096]{1,0:T(8,128)(2,1)} fusion(bf16[512,256]{1,0:T(8,128)(2,1)S(1)} %bitcast.74, bf16[512,4096]{1,0:T(8,128)(2,1)S(1)} %bitcast.65), kind=kOutput, calls=%fused_computation | convolution fusion | flops 1074790400 | bytes 6553600 | tf_op jit(solution)/shard_map/dot_general | solution.py:609
  91.1 0.1 convert_bitcast_fusion.1
  91.2 0.2 copy.38
  91.4 0.9 copy_bitcast_fusion.y_ref
  92.3 55.8 %exchange.1 = (f32[64,4096]{1,0:T(8,128)}, bf16[4,3,128,256]{3,2,1,0:T(8,128)(2,1)}, f32[4,48,256]{2,1,0:T(8,128)}) custom-call(bf16[4,64,4096]{2,1,0:T(8,128)(2,1)} %bitcast.63, bf16[4,3,128,256]{3,2,1,0:T(8,128)(2,1)} %copy_bitcast_fusion.y_ref, f32[48,256]{1,0:T(8,128)} %get-tuple-element.22.small_ref), custom_call_target="tpu_custom_call" | custom-call | tf_op jit(solution)/shard_map/exchange/pallas_call | solution.py:613
  148.1 1.5 copy.40
  149.7 0.0 copy-start.6
  149.7 0.1 fusion
  149.8 0.9 copy.48
  150.6 0.9 copy.47
  151.5 0.9 copy.46
  152.4 0.0 copy-done.6
  152.4 0.2 reshape.87
  152.6 0.8 reshape.88
  153.4 0.1 copy.45
  153.5 0.8 slice.44
  154.3 1.0 copy.58
  (22 shorter events, 0.4 us)
Async XLA Ops:
  0.6 5.9 %copy-start.5 = (bf16[1,128,1024]{2,1,0:T(8,128)(2,1)S(1)}, bf16[1,128,1024]{2,1,0:T(8,128)(2,1)}, u32[]{:S(2)}) copy-start(bf16[1,128,1024]{2,1,0:T(8,128)(2,1)} %param.10) | copy-start | bytes 786436
  0.6 5.7 %copy-start.4 = (bf16[1,128,1024]{2,1,0:T(8,128)(2,1)S(1)}, bf16[1,128,1024]{2,1,0:T(8,128)(2,1)}, u32[]{:S(2)}) copy-start(bf16[1,128,1024]{2,1,0:T(8,128)(2,1)} %param.9) | copy-start | bytes 786436
  0.7 5.5 %copy-start.3 = (bf16[1,128,1024]{2,1,0:T(8,128)(2,1)S(1)}, bf16[1,128,1024]{2,1,0:T(8,128)(2,1)}, u32[]{:S(2)}) copy-start(bf16[1,128,1024]{2,1,0:T(8,128)(2,1)} %param.8) | copy-start | bytes 786436
  3.6 3.2 %copy-start.7 = (f32[16,256]{1,0:T(8,128)}, f32[16,256]{1,0:T(8,128)S(1)}, u32[]{:S(2)}) copy-start(f32[16,256]{1,0:T(8,128)S(1)} %get-tuple-element.33.rate_row) | copy-start | bytes 49156
  48.9 2.5 %copy-start.8 = (bf16[4,64,4096]{2,1,0:T(8,128)(2,1)S(1)}, bf16[4,64,4096]{2,1,0:T(8,128)(2,1)}, u32[]{:S(2)}) copy-start(bf16[4,64,4096]{2,1,0:T(8,128)(2,1)} %get-tuple-element.19) | copy-start | bytes 6291460
  56.1 32.4 %copy-start = (bf16[4,128,4096]{2,1,0:T(8,128)(2,1)S(1)}, bf16[4,128,4096]{2,1,0:T(8,128)(2,1)}, u32[]{:S(2)}) copy-start(bf16[4,128,4096]{2,1,0:T(8,128)(2,1)} %get-tuple-element.18) | copy-start | bytes 12582916
  88.5 2.6 %copy-start.1 = (f32[3,64,8,256]{3,2,1,0:T(8,128)S(1)}, f32[3,64,8,256]{3,2,1,0:T(8,128)}, u32[]{:S(2)}) copy-start(f32[3,64,8,256]{3,2,1,0:T(8,128)} %get-tuple-element.21) | copy-start | bytes 4718596
  149.7 2.7 %copy-start.6 = (f32[4,48,256]{2,1,0:T(8,128)S(1)}, f32[4,48,256]{2,1,0:T(8,128)}, u32[]{:S(2)}) copy-start(f32[4,48,256]{2,1,0:T(8,128)} %get-tuple-element.25) | copy-start | bytes 589828
  150.6 3.7 %copy-start.2 = (f32[64,4096]{1,0:T(8,128)S(1)}, f32[64,4096]{1,0:T(8,128)}, u32[]{:S(2)}) copy-start(f32[64,4096]{1,0:T(8,128)} %get-tuple-element.48) | copy-start | bytes 3145732

commit v3 on v2

--- a/solution.py
+++ b/solution.py
@@ -165,17 +165,21 @@
 
 
 def scan_kernel(
-    group, count, x_ref, up_ref, taps_row, factor_row, coef_row, rate_row, norm_ref,
-    y_ref, gated_ref, small_ref, taps_ref, factor_ref, coef_ref,
+    group, count, rows_dp, x_ref, up_ref, taps_row, factor_row, coef_row, rate_row, norm_ref,
+    go_ref, wg_ref, yo_ref, so_ref, taps_ref, factor_ref, coef_ref,
     shaped, mixed, gradf, gext, starts, bstarts, states, hsend, hrecv,
-    ss, sr, hss, hsr,
+    gated_ref, gated_t, small_ref, wp_ref, y_ref,
+    wbuf, pair, qbuf, qsum, qz, qpair, sbuf,
+    ss, sr, hss, hsr, wsend, wrecv, ysend, yrecv, ssend, srecv, tsend, trecv, psend, precv,
+    qsend, qrecv, zsend, zrecv, fsend, frecv, own,
 ):
     me = lax.axis_index("ctx")
+    line = lax.axis_index("dp")
     mine, block = lax.rem(me, group), lax.div(me, group)
     steps = up_ref.shape[0]
     width = up_ref.shape[2]
     modes = factor_ref.shape[0]
-    greet_all(group * count, 1)
+    greet_all(group * count, rows_dp)
     for m in range(modes):
         factor_ref[m] = jnp.broadcast_to(factor_row[m : m + 1], (CHUNKS, width))
         coef_ref[m] = jnp.broadcast_to(coef_row[m : m + 1], (CHUNKS, width))
@@ -268,98 +272,16 @@
             return new
 
         lax.fori_loop(0, steps, second, tuple(starts[m, :, span] for m in range(modes)))
-
-        def second_back(k, carry):
-            state, total = carry
-            s = steps - 1 - k
-            value = gradf[s, :, span]
-            other = mixed[s, :, span]
-            new = tuple(factor_ref[m, :, span] * state[m] + value for m in range(modes))
-            total = tuple(total[m] + other * new[m] for m in range(modes))
-            grad = tree_sum([coef_ref[m, :, span] * new[m] for m in range(modes)])
-            gext[1, s, :, span] = grad * shaped[2, s, :, span]
-            gext[2, s, :, span] = grad * shaped[1, s, :, span]
-            return new, total
-
-        _, total = lax.fori_loop(
-            0, steps, second_back, (tuple(bstarts[m, :, span] for m in range(modes)), zeros)
-        )
-        for m in range(modes):
-            small_ref[21 + m : 22 + m, span] = norm_ref[m : m + 1, span] * jnp.sum(
-                total[m], axis=0, keepdims=True
-            )
-    small_ref[21 + modes :, :] = jnp.zeros((small_ref.shape[0] - 21 - modes, width), jnp.float32)
-
-    for i in range(3):
-        for s in range(HALO):
-            hsend[i, s : s + 1, :] = gext[i, s, 0:1, :]
-    ahead = remote(
-        hsend, hrecv, hss.at[0], hsr.at[0], jnp.maximum(block - 1, 0) * group + mine
-    )
-
-    @pl.when(block > 0)
-    def _():
-        ahead.start()
-
-    for span in spans:
-        for i in range(3):
-
-            def tap(s, sums):
-                value = gext[i, s, :, span]
-                return tuple(
-                    sums[j] + value * x_ref[i, s + HALO - j, :, span] for j in range(7)
-                )
-
-            sums = lax.fori_loop(0, steps, tap, zeros[:7], unroll=2)
-            for j in range(7):
-                at = i * 7 + j
-                small_ref[at : at + 1, span] = jnp.sum(sums[j], axis=0, keepdims=True)
-
-    @pl.when(block == count - 1)
-    def _():
-        hrecv[...] = jnp.zeros_like(hrecv)
-
-    @pl.when(block > 0)
-    def _():
-        ahead.wait_send()
-
-    @pl.when(block < count - 1)
-    def _():
-        ahead.wait_recv()
-
-    for span in spans:
-        for i in range(3):
-            for s in range(HALO):
-                gext[i, steps + s, :, span] = jnp.where(
-                    row < CHUNKS - 1,
-                    pltpu.roll(gext[i, s, :, span], CHUNKS - 1, 0),
-                    hrecv[i, s : s + 1, span],
-                )
-
-            def out(s, nothing):
-                y_ref[i, s, :, span] = tree_sum(
-                    [taps_ref[i, j, :, span] * gext[i, s + j, :, span] for j in range(7)]
-                )
-                return nothing
-
-            lax.fori_loop(0, steps, out, 0, unroll=2)
-
-
-def exchange_kernel(
-    group, count, rows_dp, wp_ref, y_ref, small_ref, wg_ref, yo_ref, so_ref,
-    wbuf, pair, qbuf, qsum, qz, qpair, sbuf,
-    wsend, wrecv, ysend, yrecv, ssend, srecv, tsend, trecv, psend, precv,
-    qsend, qrecv, zsend, zrecv, fsend, frecv, own,
-):
-    me, row = lax.axis_index("ctx"), lax.axis_index("dp")
-    mine, block = lax.rem(me, group), lax.div(me, group)
+        gated_t[span, :] = jnp.swapaxes(
+            jnp.swapaxes(gated_ref[:, :, span], 0, 1).reshape(steps * CHUNKS, LANES), 0, 1
+        ).astype(gated_t.dtype)
+
     f32 = jnp.float32
     half = pair.shape[2]
     part = qpair.shape[2]
     tile = math.gcd(part, 512)
-    greet_all(group * count, rows_dp)
     members = count * rows_dp
-    slot = block * rows_dp + row
+    slot = block * rows_dp + line
     smalls = []
     for step in range(1, members):
         there = lax.rem(slot + step, members)
@@ -386,7 +308,7 @@
         sums.append(remote(qsum.at[there], qz.at[step], zsend.at[step], zrecv.at[step], to))
     quarters, pairs, finals = [], [], []
     for step in range(1, rows_dp):
-        to = lax.rem(row + step, rows_dp)
+        to = lax.rem(line + step, rows_dp)
         columns = pl.ds(pl.multiple_of(half + to * part, part), part)
         quarters.append(
             remote(
@@ -394,10 +316,10 @@
             )
         )
         pairs.append(
-            remote(pair.at[row], pair.at[row], psend.at[step], precv.at[step], me, to)
+            remote(pair.at[line], pair.at[line], psend.at[step], precv.at[step], me, to)
         )
         finals.append(
-            remote(qpair.at[row], qpair.at[row], fsend.at[step], frecv.at[step], me, to)
+            remote(qpair.at[line], qpair.at[line], fsend.at[step], frecv.at[step], me, to)
         )
     outs, totals = [], []
     for step in range(1, group):
@@ -409,12 +331,6 @@
         totals.append(
             remote(so_ref.at[mine], so_ref.at[mine], tsend.at[step], trecv.at[step], to)
         )
-    for copy in quarters + weights + outs + smalls:
-        copy.start()
-    keep = pltpu.make_async_copy(y_ref.at[mine], yo_ref.at[mine], own.at[0])
-    keep.start()
-    sbuf[slot] = small_ref[...]
-
     def each(width, body):
         def run(k, nothing):
             body(pl.multiple_of(k * tile, tile))
@@ -422,11 +338,82 @@
 
         lax.fori_loop(0, width // tile, run, 0)
 
+
+    own_rows = wp_ref.shape[1]
+
+    def product(at):
+        at = pl.ds(at, tile)
+        value = jnp.dot(gated_t[...], go_ref[:, at], preferred_element_type=f32)
+        value = value.astype(wp_ref.dtype)
+        for k in range(count):
+            wp_ref[k, :, at] = value[k * own_rows : (k + 1) * own_rows]
+
+    each(half, lambda at: product(pl.multiple_of(half + at, tile)))
     for copy in quarters:
+        copy.start()
+    each(half, product)
+    for copy in weights:
+        copy.start()
+
+    for span in spans:
+
+        def second_back(k, carry):
+            state, total = carry
+            s = steps - 1 - k
+            value = gradf[s, :, span]
+            other = mixed[s, :, span]
+            new = tuple(factor_ref[m, :, span] * state[m] + value for m in range(modes))
+            total = tuple(total[m] + other * new[m] for m in range(modes))
+            grad = tree_sum([coef_ref[m, :, span] * new[m] for m in range(modes)])
+            gext[1, s, :, span] = grad * shaped[2, s, :, span]
+            gext[2, s, :, span] = grad * shaped[1, s, :, span]
+            return new, total
+
+        _, total = lax.fori_loop(
+            0, steps, second_back, (tuple(bstarts[m, :, span] for m in range(modes)), zeros)
+        )
+        for m in range(modes):
+            small_ref[21 + m : 22 + m, span] = norm_ref[m : m + 1, span] * jnp.sum(
+                total[m], axis=0, keepdims=True
+            )
+    if small_ref.shape[0] > 21 + modes:
+        small_ref[21 + modes :, :] = jnp.zeros(
+            (small_ref.shape[0] - 21 - modes, width), jnp.float32
+        )
+
+    for i in range(3):
+        for s in range(HALO):
+            hsend[i, s : s + 1, :] = gext[i, s, 0:1, :]
+    ahead = remote(
+        hsend, hrecv, hss.at[0], hsr.at[0], jnp.maximum(block - 1, 0) * group + mine
+    )
+
+    @pl.when(block > 0)
+    def _():
+        ahead.start()
+
+    for span in spans:
+        for i in range(3):
+
+            def tap(s, sums):
+                value = gext[i, s, :, span]
+                return tuple(
+                    sums[j] + value * x_ref[i, s + HALO - j, :, span] for j in range(7)
+                )
+
+            tapped = lax.fori_loop(0, steps, tap, zeros[:7], unroll=2)
+            for j in range(7):
+                at = i * 7 + j
+                small_ref[at : at + 1, span] = jnp.sum(tapped[j], axis=0, keepdims=True)
+
+    sbuf[slot] = small_ref[...]
+    for copy in smalls:
+        copy.start()
+    for copy in quarters:
         copy.wait()
 
     def add_rows(at):
-        source = pl.ds(pl.multiple_of(half + row * part + at, tile), tile)
+        source = pl.ds(pl.multiple_of(half + line * part + at, tile), tile)
         at = pl.ds(at, tile)
         for k in range(count):
             value = wp_ref[k, :, source].astype(f32)
@@ -437,6 +424,42 @@
     each(part, add_rows)
     for copy in sums:
         copy.start()
+
+    @pl.when(block == count - 1)
+    def _():
+        hrecv[...] = jnp.zeros_like(hrecv)
+
+    @pl.when(block > 0)
+    def _():
+        ahead.wait_send()
+
+    @pl.when(block < count - 1)
+    def _():
+        ahead.wait_recv()
+
+    for span in spans:
+        for i in range(3):
+            for s in range(HALO):
+                gext[i, steps + s, :, span] = jnp.where(
+                    row < CHUNKS - 1,
+                    pltpu.roll(gext[i, s, :, span], CHUNKS - 1, 0),
+                    hrecv[i, s : s + 1, span],
+                )
+
+            def out(s, nothing):
+                shaped[i, s, :, span] = tree_sum(
+                    [taps_ref[i, j, :, span] * gext[i, s + j, :, span] for j in range(7)]
+                )
+                return nothing
+
+            lax.fori_loop(0, steps, out, 0, unroll=2)
+            value = jnp.swapaxes(shaped[i, :, :, span], 0, 1).astype(y_ref.dtype)
+            y_ref[:, i, :, span] = value.reshape(group, y_ref.shape[2], LANES)
+
+    for copy in outs:
+        copy.start()
+    keep = pltpu.make_async_copy(y_ref.at[mine], yo_ref.at[mine], own.at[0])
+    keep.start()
     for copy in smalls:
         copy.wait()
     total = sbuf[0]
@@ -453,7 +476,7 @@
         value = wp_ref[block, :, at].astype(f32)
         for step in range(1, count):
             value = value + wbuf[step, :, at].astype(f32)
-        pair[row, :, at] = value.astype(pair.dtype)
+        pair[line, :, at] = value.astype(pair.dtype)
 
     each(half, add)
     for copy in pairs:
@@ -466,7 +489,7 @@
         value = qsum[block, :, at].astype(f32)
         for step in range(1, count):
             value = value + qz[step, :, at].astype(f32)
-        qpair[row, :, at] = value.astype(qpair.dtype)
+        qpair[line, :, at] = value.astype(qpair.dtype)
 
     each(part, add_blocks)
     for copy in finals:
@@ -569,14 +592,16 @@
     rate = picked(decay_rate.T)
     norm = jnp.sqrt(-jnp.expm1(-2.0 * rate))
     coef = picked(residues.T) * norm
-    y, gated, small = pl.pallas_call(
-        functools.partial(scan_kernel, group, count),
+    tall = (21 + modes + 7) // 8 * 8
+    small = (tall, width)
+    weight_grad, yo, so = pl.pallas_call(
+        functools.partial(scan_kernel, group, count, rows_dp),
         out_shape=(
-            jax.ShapeDtypeStruct((3, steps, CHUNKS, width), f32),
-            jax.ShapeDtypeStruct((steps, CHUNKS, width), f32),
-            jax.ShapeDtypeStruct(((21 + modes + 7) // 8 * 8 + 8, width), f32),
+            jax.ShapeDtypeStruct((own_rows, columns), f32),
+            jax.ShapeDtypeStruct((group, 3, tokens, width), bf16),
+            jax.ShapeDtypeStruct((group,) + small, f32),
         ),
-        in_specs=[VMEM] * 7,
+        in_specs=[VMEM] * 8,
         out_specs=(VMEM,) * 3,
         scratch_shapes=[
             pltpu.VMEM((3, 7, CHUNKS, width), f32),
@@ -591,51 +616,28 @@
             pltpu.VMEM((count, 2, modes, width), f32),
             pltpu.VMEM((3, HALO, width), f32),
             pltpu.VMEM((3, HALO, width), f32),
-            DMA((count,)), DMA((count,)), DMA((1,)), DMA((1,)),
-        ],
-        compiler_params=params(1),
-        name="scan",
-    )(
-        extended,
-        upstream,
-        taps,
-        jnp.exp(-rate),
-        coef,
-        rate,
-        norm,
-    )
-
-    gated = jnp.swapaxes(gated, 0, 1).reshape(span_tokens, width).astype(bf16)
-    partial = lax.dot_general(
-        gated, out_rows, (((0,), (0,)), ((), ())), preferred_element_type=f32
-    ).astype(bf16)
-    y = jnp.swapaxes(y.astype(bf16), 1, 2).reshape(3, group, tokens, width)
-    weight_grad, yo, so = pl.pallas_call(
-        functools.partial(exchange_kernel, group, count, rows_dp),
-        out_shape=(
-            jax.ShapeDtypeStruct((own_rows, columns), f32),
-            jax.ShapeDtypeStruct((group, 3, tokens, width), bf16),
-            jax.ShapeDtypeStruct((group,) + small.shape, f32),
-        ),
-        in_specs=[VMEM] * 3,
-        out_specs=(VMEM,) * 3,
-        scratch_shapes=[
+            pltpu.VMEM((steps, CHUNKS, width), f32),
+            pltpu.VMEM((width, span_tokens), bf16),
+            pltpu.VMEM(small, f32),
+            pltpu.VMEM((count, own_rows, columns), bf16),
+            pltpu.VMEM((group, 3, tokens, width), bf16),
             pltpu.VMEM((count, own_rows, half), bf16),
             pltpu.VMEM((rows_dp, own_rows, half), bf16),
             pltpu.VMEM((rows_dp, count, own_rows, part), bf16),
             pltpu.VMEM((count, own_rows, part), bf16),
             pltpu.VMEM((count, own_rows, part), bf16),
             pltpu.VMEM((rows_dp, own_rows, part), bf16),
-            pltpu.VMEM((count * rows_dp,) + small.shape, f32),
+            pltpu.VMEM((count * rows_dp,) + small, f32),
+            DMA((count,)), DMA((count,)), DMA((1,)), DMA((1,)),
             DMA((count,)), DMA((count,)), DMA((group,)), DMA((group,)),
             DMA((count * rows_dp,)), DMA((count * rows_dp,)),
             DMA((group,)), DMA((group,)), DMA((rows_dp,)), DMA((rows_dp,)),
             DMA((rows_dp,)), DMA((rows_dp,)), DMA((count,)), DMA((count,)),
             DMA((rows_dp,)), DMA((rows_dp,)), DMA((1,)),
         ],
-        compiler_params=params(2),
-        name="exchange",
-    )(partial.reshape(count, own_rows, columns), jnp.swapaxes(y, 0, 1), small)
+        compiler_params=params(1),
+        name="scan",
+    )(extended, upstream, taps, jnp.exp(-rate), coef, rate, norm, out_rows)
 
     def joined(v):
         v = v.reshape(v.shape[:-1] + (count, own_rows))

time: 156 us -> 139 us (0.89)
  Pallas kernels: 127 us -> 115 us
  matrix products: 6.09 us -> 3.47 us
    pallas_call x2 -> x1, Pallas kernels: 85.7 us -> 74.1 us  [shards(): pl.pallas_call(functools.partial(scan_kernel, group, count, rows_dp), out...]
    dot_general x1 -> x0, matrix products: 2.62 us -> none  [shards(): lax.dot_general(gated, out_rows, (((0,), (0,)), ((), ())), preferred_elem...]
    unnamed x26 -> x22, local copies, waits for them, and re-layouts: 4.67 us -> 4.67 us
where the time goes in v3:
time: 139 us
  Pallas kernels  115 us (83%)
  local copies, waits for them, and re-layouts  16.6 us (12%)
  matrix products  3.47 us (2%)
  other arithmetic  2.76 us (2%)
    pallas_call x1, Pallas kernels, shards(): pl.pallas_call(functools.partial(scan_kernel, group, count, rows_dp), out...  74.1 us
    pallas_call x1, Pallas kernels, shards(): pl.pallas_call(functools.partial(gather_kernel, group, count, rows_dp), o...  40.9 us
    unnamed x22, local copies, waits for them, and re-layouts  4.67 us
    dot_general x1, matrix products, shards(): lax.dot_general(out_rows, wg.reshape(width, columns), (((1,), (1,)), ((),...  3.47 us
    reshape x4, local copies, waits for them, and re-layouts, parted(): v = v.reshape(v.shape[:-1] + (count, group, own_rows))  3.06 us

profile of v3, /device:TPU:8, one launch (start us, length us, event | category | flops | bytes accessed | tf_op | source)
XLA Modules:
  0.0 138.8 jit_solution(7825885165447871654)
XLA Ops:
  0.6 0.0 copy-start.3
  0.6 0.0 copy-start.2
  0.7 0.0 copy-start.1
  0.7 1.0 reshape.73
  1.7 0.1 reshape.74
  1.9 1.0 reshape.71
  2.9 0.1 reshape.72
  3.0 0.6 negate_sqrt_fusion
  3.6 0.0 copy-start.5
  3.6 0.6 bitcast_multiply_fusion
  4.3 1.0 reshape.69
  5.4 0.1 reshape.70
  5.5 0.6 copy.52
  6.1 0.0 copy-done.1
  6.1 0.2 copy.24
  6.3 0.0 copy-done.2
  6.3 0.2 copy.25
  6.5 0.0 copy-done.3
  6.5 0.2 copy.26
  6.7 0.1 pad_maximum_fusion
  6.8 0.1 copy.27
  6.8 0.0 copy-done.5
  6.8 1.2 copy.28.x_ref
  8.0 40.9 %gather.1 = (bf16[4,3,128,256]{3,2,1,0:T(8,128)(2,1)}, bf16[4,128,4096]{2,1,0:T(8,128)(2,1)}, bf16[4,64,4096]{2,1,0:T(8,128)(2,1)}, bf16[3,16,256]{2,1,0:T(8,128)(2,1)}) custom-call(bf16[4,3,128,256]{3,2,1,0:T(8,128)(2,1)} %copy.28.x_ref, bf16[128,4096]{1,0:T(8,128)(2,1)} %bitcast.57, bf16[64,4096]{1,0:T(8,128)(2,1)} %w_ref.1), custom_call_target="tpu_custom_call" | custom-call | tf_op jit(solution)/shard_map/gather/pallas_call | solution.py:557
  49.0 0.0 copy-start.6
  49.0 0.9 slice_bitcast_fusion
  49.8 1.2 copy.29
  51.0 0.4 copy.30
  51.5 0.0 copy-done.6
  51.5 3.5 %fusion.1 = f32[8,64,256]{2,1,0:T(8,128)S(1)} fusion(bf16[8,64,4096]{2,1,0:T(8,128)(2,1)} %bitcast.48, bf16[256,4096,1]{1,0,2:T(8,128)(2,1)S(1)} %bitcast.71), kind=kOutput, calls=%fused_computation.12 | convolution fusion | flops 1073741824 | bytes 6815744 | tf_op jit(solution)/shard_map/dot_general | solution.py:578
  55.0 1.1 copy.50
  56.1 1.4 %convert_bitcast_fusion.x_ref = f32[3,72,8,256]{3,2,1,0:T(8,128)} fusion(bf16[3,8,64,256]{3,1,2,0:T(8,128)(2,1)S(1)} %copy.30, bf16[3,7,8,256]{3,1,2,0:T(8,128)(2,1)S(1)} %slice.45, bf16[3,1,8,256]{3,1,2,0:T(2,128)(2,1)S(1)} %copy.31), kind=kLoop, calls=%fused_computation | loop fusion | flops 2654208 | bytes 2654208 | tf_op jit(solution)/shard_map/convert_element_type | solution.py:589
  57.5 74.1 %scan.1 = (f32[64,4096]{1,0:T(8,128)}, bf16[4,3,128,256]{3,2,1,0:T(8,128)(2,1)}, f32[4,40,256]{2,1,0:T(8,128)}) custom-call(f32[3,72,8,256]{3,2,1,0:T(8,128)} %convert_bitcast_fusion.x_ref, f32[64,8,256]{2,1,0:T(8,128)} %bitcast.54, f32[3,7,256]{2,1,0:T(8,128)} %bitcast.65, f32[16,256]{1,0:T(8,128)} %get-tuple-element.32.factor_row, ...), custom_call_target="tpu_custom_call" | custom-call | tf_op jit(solution)/shard_map/scan/pallas_call | solution.py:597
  131.6 1.5 %copy.37 = bf16[4,3,128,256]{2,3,1,0:T(8,128)(2,1)S(1)} copy(bf16[4,3,128,256]{3,2,1,0:T(8,128)(2,1)} %get-tuple-element.17) | data formatting | bytes 1572864 | tf_op jit(solution)/shard_map/scan/pallas_call | solution.py:597
  133.2 0.0 copy-start.4
  133.2 0.1 fusion
  133.3 0.9 copy.45
  134.1 0.0 copy-start
  134.1 0.9 copy.44
  135.0 0.9 copy.43
  135.9 0.0 copy-done.4
  135.9 0.2 reshape.77
  136.1 0.8 reshape.78
  136.9 0.1 copy.42
  137.0 0.8 slice.44
  137.8 0.0 copy-done
  137.8 1.0 copy.54
  (12 shorter events, 0.3 us)
Async XLA Ops:
  0.6 5.9 %copy-start.3 = (bf16[1,128,1024]{2,1,0:T(8,128)(2,1)S(1)}, bf16[1,128,1024]{2,1,0:T(8,128)(2,1)}, u32[]{:S(2)}) copy-start(bf16[1,128,1024]{2,1,0:T(8,128)(2,1)} %param.10) | copy-start | bytes 786436
  0.6 5.7 %copy-start.2 = (bf16[1,128,1024]{2,1,0:T(8,128)(2,1)S(1)}, bf16[1,128,1024]{2,1,0:T(8,128)(2,1)}, u32[]{:S(2)}) copy-start(bf16[1,128,1024]{2,1,0:T(8,128)(2,1)} %param.9) | copy-start | bytes 786436
  0.7 5.5 %copy-start.1 = (bf16[1,128,1024]{2,1,0:T(8,128)(2,1)S(1)}, bf16[1,128,1024]{2,1,0:T(8,128)(2,1)}, u32[]{:S(2)}) copy-start(bf16[1,128,1024]{2,1,0:T(8,128)(2,1)} %param.8) | copy-start | bytes 786436
  3.6 3.2 %copy-start.5 = (f32[16,256]{1,0:T(8,128)}, f32[16,256]{1,0:T(8,128)S(1)}, u32[]{:S(2)}) copy-start(f32[16,256]{1,0:T(8,128)S(1)} %get-tuple-element.27.rate_row) | copy-start | bytes 49156
  49.0 2.5 %copy-start.6 = (bf16[4,64,4096]{2,1,0:T(8,128)(2,1)S(1)}, bf16[4,64,4096]{2,1,0:T(8,128)(2,1)}, u32[]{:S(2)}) copy-start(bf16[4,64,4096]{2,1,0:T(8,128)(2,1)} %get-tuple-element.16) | copy-start | bytes 6291460
  133.2 2.7 %copy-start.4 = (f32[4,40,256]{2,1,0:T(8,128)S(1)}, f32[4,40,256]{2,1,0:T(8,128)}, u32[]{:S(2)}) copy-start(f32[4,40,256]{2,1,0:T(8,128)} %get-tuple-element.19) | copy-start | bytes 491524
  134.1 3.7 %copy-start = (f32[64,4096]{1,0:T(8,128)S(1)}, f32[64,4096]{1,0:T(8,128)}, u32[]{:S(2)}) copy-start(f32[64,4096]{1,0:T(8,128)} %get-tuple-element.42) | copy-start | bytes 3145732

commit v4 on v3

--- a/solution.py
+++ b/solution.py
@@ -12,6 +12,7 @@
 CHUNKS = 8
 HALO = 8
 PIECES = 4
+ROUNDS = 3
 
 
 def at_device(ctx, dp=None):
@@ -278,7 +279,7 @@
 
     f32 = jnp.float32
     half = pair.shape[2]
-    part = qpair.shape[2]
+    part = qpair.shape[3]
     tile = math.gcd(part, 512)
     members = count * rows_dp
     slot = block * rows_dp + line
@@ -295,7 +296,7 @@
                 lax.rem(there, rows_dp),
             )
         )
-    weights, sums = [], []
+    weights = []
     for step in range(1, count):
         there = lax.rem(block + step, count)
         to = there * group + mine
@@ -305,22 +306,36 @@
                 wrecv.at[step], to,
             )
         )
-        sums.append(remote(qsum.at[there], qz.at[step], zsend.at[step], zrecv.at[step], to))
-    quarters, pairs, finals = [], [], []
+    pairs = []
+    quarters, finals = [[] for _ in range(ROUNDS)], [[] for _ in range(ROUNDS)]
+    sums = [[] for _ in range(ROUNDS)]
     for step in range(1, rows_dp):
         to = lax.rem(line + step, rows_dp)
-        columns = pl.ds(pl.multiple_of(half + to * part, part), part)
-        quarters.append(
-            remote(
-                wp_ref.at[:, :, columns], qbuf.at[step], qsend.at[step], qrecv.at[step], me, to
-            )
-        )
         pairs.append(
             remote(pair.at[line], pair.at[line], psend.at[step], precv.at[step], me, to)
         )
-        finals.append(
-            remote(qpair.at[line], qpair.at[line], fsend.at[step], frecv.at[step], me, to)
-        )
+        for q in range(ROUNDS):
+            begin = half + q * rows_dp * part
+            columns = pl.ds(pl.multiple_of(begin + to * part, part), part)
+            at = q * rows_dp + step
+            quarters[q].append(
+                remote(
+                    wp_ref.at[:, :, columns], qbuf.at[q, step], qsend.at[at], qrecv.at[at],
+                    me, to,
+                )
+            )
+            held = qpair.at[q, line]
+            finals[q].append(remote(held, held, fsend.at[at], frecv.at[at], me, to))
+    for step in range(1, count):
+        there = lax.rem(block + step, count)
+        for q in range(ROUNDS):
+            at = q * count + step
+            sums[q].append(
+                remote(
+                    qsum.at[q, there], qz.at[q, step], zsend.at[at], zrecv.at[at],
+                    there * group + mine,
+                )
+            )
     outs, totals = [], []
     for step in range(1, group):
         there = lax.rem(mine + step, group)
@@ -348,12 +363,11 @@
         for k in range(count):
             wp_ref[k, :, at] = value[k * own_rows : (k + 1) * own_rows]
 
-    each(half, lambda at: product(pl.multiple_of(half + at, tile)))
-    for copy in quarters:
-        copy.start()
-    each(half, product)
-    for copy in weights:
-        copy.start()
+    for q in (0, ROUNDS) + tuple(range(1, ROUNDS)):
+        begin = half + q * rows_dp * part if q < ROUNDS else 0
+        each(half, lambda at: product(pl.multiple_of(begin + at, tile)))
+        for copy in quarters[q] if q < ROUNDS else weights:
+            copy.start()
 
     for span in spans:
 
@@ -409,21 +423,26 @@
     sbuf[slot] = small_ref[...]
     for copy in smalls:
         copy.start()
-    for copy in quarters:
-        copy.wait()
-
-    def add_rows(at):
-        source = pl.ds(pl.multiple_of(half + line * part + at, tile), tile)
-        at = pl.ds(at, tile)
-        for k in range(count):
-            value = wp_ref[k, :, source].astype(f32)
-            for step in range(1, rows_dp):
-                value = value + qbuf[step, k, :, at].astype(f32)
-            qsum[k, :, at] = value.astype(qsum.dtype)
-
-    each(part, add_rows)
-    for copy in sums:
-        copy.start()
+    def gather_rows(q):
+        for copy in quarters[q]:
+            copy.wait()
+
+        def add_rows(at):
+            begin = half + q * rows_dp * part
+            source = pl.ds(pl.multiple_of(begin + line * part + at, tile), tile)
+            at = pl.ds(at, tile)
+            for k in range(count):
+                value = wp_ref[k, :, source].astype(f32)
+                for step in range(1, rows_dp):
+                    value = value + qbuf[q, step, k, :, at].astype(f32)
+                qsum[q, k, :, at] = value.astype(qsum.dtype)
+
+        each(part, add_rows)
+        for copy in sums[q]:
+            copy.start()
+
+    for q in range(ROUNDS - 1):
+        gather_rows(q)
 
     @pl.when(block == count - 1)
     def _():
@@ -456,6 +475,8 @@
             value = jnp.swapaxes(shaped[i, :, :, span], 0, 1).astype(y_ref.dtype)
             y_ref[:, i, :, span] = value.reshape(group, y_ref.shape[2], LANES)
 
+    for q in range(ROUNDS - 1, ROUNDS):
+        gather_rows(q)
     for copy in outs:
         copy.start()
     keep = pltpu.make_async_copy(y_ref.at[mine], yo_ref.at[mine], own.at[0])
@@ -481,19 +502,23 @@
     each(half, add)
     for copy in pairs:
         copy.start()
-    for copy in sums:
-        copy.wait()
-
-    def add_blocks(at):
-        at = pl.ds(at, tile)
-        value = qsum[block, :, at].astype(f32)
-        for step in range(1, count):
-            value = value + qz[step, :, at].astype(f32)
-        qpair[line, :, at] = value.astype(qpair.dtype)
-
-    each(part, add_blocks)
-    for copy in finals:
-        copy.start()
+    def gather_blocks(q):
+        for copy in sums[q]:
+            copy.wait()
+
+        def add_blocks(at):
+            at = pl.ds(at, tile)
+            value = qsum[q, block, :, at].astype(f32)
+            for step in range(1, count):
+                value = value + qz[q, step, :, at].astype(f32)
+            qpair[q, line, :, at] = value.astype(qpair.dtype)
+
+        each(part, add_blocks)
+        for copy in finals[q]:
+            copy.start()
+
+    for q in range(ROUNDS):
+        gather_blocks(q)
     for copy in pairs:
         copy.wait()
 
@@ -505,15 +530,17 @@
         wg_ref[:, at] = value
 
     each(half, finish)
-    for copy in finals:
-        copy.wait()
-    for other in range(rows_dp):
-
-        def finish_part(at):
-            to = pl.ds(pl.multiple_of(half + other * part + at, tile), tile)
-            wg_ref[:, to] = qpair[other, :, pl.ds(at, tile)].astype(f32)
-
-        each(part, finish_part)
+    for q in range(ROUNDS):
+        for copy in finals[q]:
+            copy.wait()
+        for other in range(rows_dp):
+
+            def finish_part(at):
+                begin = half + (q * rows_dp + other) * part
+                to = pl.ds(pl.multiple_of(begin + at, tile), tile)
+                wg_ref[:, to] = qpair[q, other, :, pl.ds(at, tile)].astype(f32)
+
+            each(part, finish_part)
     keep.wait()
     for copy in outs + totals:
         copy.wait()
@@ -543,7 +570,7 @@
     span_tokens = group * tokens
     steps = span_tokens // CHUNKS
     f32, bf16 = jnp.float32, jnp.bfloat16
-    half = columns // 2
+    half = columns // (ROUNDS + 1)
     part = half // rows_dp
 
     def parted(v):
@@ -588,10 +615,19 @@
     )
     extended = jnp.swapaxes(jnp.concatenate([before, whole], axis=2), 1, 2).astype(f32)
 
-    taps = picked(jnp.swapaxes(short_taps, 1, 2))
-    rate = picked(decay_rate.T)
+    tables = picked(
+        jnp.concatenate(
+            [
+                jnp.swapaxes(short_taps, 1, 2).reshape(21, channels),
+                residues.T,
+                decay_rate.T,
+            ]
+        )
+    )
+    taps = tables[:21].reshape(3, 7, width)
+    rate = tables[21 + modes :]
     norm = jnp.sqrt(-jnp.expm1(-2.0 * rate))
-    coef = picked(residues.T) * norm
+    coef = tables[21 : 21 + modes] * norm
     tall = (21 + modes + 7) // 8 * 8
     small = (tall, width)
     weight_grad, yo, so = pl.pallas_call(
@@ -623,17 +659,18 @@
             pltpu.VMEM((group, 3, tokens, width), bf16),
             pltpu.VMEM((count, own_rows, half), bf16),
             pltpu.VMEM((rows_dp, own_rows, half), bf16),
-            pltpu.VMEM((rows_dp, count, own_rows, part), bf16),
-            pltpu.VMEM((count, own_rows, part), bf16),
-            pltpu.VMEM((count, own_rows, part), bf16),
-            pltpu.VMEM((rows_dp, own_rows, part), bf16),
+            pltpu.VMEM((ROUNDS, rows_dp, count, own_rows, part), bf16),
+            pltpu.VMEM((ROUNDS, count, own_rows, part), bf16),
+            pltpu.VMEM((ROUNDS, count, own_rows, part), bf16),
+            pltpu.VMEM((ROUNDS, rows_dp, own_rows, part), bf16),
             pltpu.VMEM((count * rows_dp,) + small, f32),
             DMA((count,)), DMA((count,)), DMA((1,)), DMA((1,)),
             DMA((count,)), DMA((count,)), DMA((group,)), DMA((group,)),
             DMA((count * rows_dp,)), DMA((count * rows_dp,)),
             DMA((group,)), DMA((group,)), DMA((rows_dp,)), DMA((rows_dp,)),
-            DMA((rows_dp,)), DMA((rows_dp,)), DMA((count,)), DMA((count,)),
-            DMA((rows_dp,)), DMA((rows_dp,)), DMA((1,)),
+            DMA((ROUNDS * rows_dp,)), DMA((ROUNDS * rows_dp,)),
+            DMA((ROUNDS * count,)), DMA((ROUNDS * count,)),
+            DMA((ROUNDS * rows_dp,)), DMA((ROUNDS * rows_dp,)), DMA((1,)),
         ],
         compiler_params=params(1),
         name="scan",

time: 139 us -> 132 us (0.950); the launches traced: 139 us -> 130 us
  Pallas kernels: 115 us -> 106 us
    pallas_call x1, Pallas kernels: 74.1 us -> 65.5 us  [shards(): pl.pallas_call(functools.partial(scan_kernel, group, count, rows_dp), out...]
    concatenate x0 -> x6, local copies, waits for them, and re-layouts: none -> 3.15 us  [shards(): jnp.concatenate([jnp.swapaxes(short_taps, 1, 2).reshape(21, channels), re...]
    reshape x4 -> x1, local copies, waits for them, and re-layouts: 3.06 us -> 0.61 us  [shards(): taps = tables[:21].reshape(3, 7, width)]
    unnamed x22 -> x21, local copies, waits for them, and re-layouts: 4.67 us -> 4.05 us
where the time goes in v4:
time: 132 us; the launch traced here: 130 us
  Pallas kernels  106 us (80%)
  local copies, waits for them, and re-layouts  16.4 us (12%)
  matrix products  3.47 us (3%)
  other arithmetic  2.88 us (2%)
    pallas_call x1, Pallas kernels, shards(): pl.pallas_call(functools.partial(scan_kernel, group, count, rows_dp), out...  65.5 us
    pallas_call x1, Pallas kernels, shards(): pl.pallas_call(functools.partial(gather_kernel, group, count, rows_dp), o...  40.9 us
    unnamed x21, local copies, waits for them, and re-layouts  4.05 us
    dot_general x1, matrix products, shards(): lax.dot_general(out_rows, wg.reshape(width, columns), (((1,), (1,)), ((),...  3.47 us
    concatenate x6, local copies, waits for them, and re-layouts, shards(): jnp.concatenate([jnp.swapaxes(short_taps, 1, 2).reshape(21, channels), re...  3.15 us

profile of v4, /device:TPU:8, one launch (start us, length us, event | category | flops | bytes accessed | tf_op | source)
XLA Modules:
  0.0 130.1 jit_solution(6113305497654906304)
XLA Ops:
  0.6 0.0 copy-start.2
  0.6 0.0 copy-start.1
  0.7 1.0 concatenate.19
  1.7 0.0 copy-start.3
  1.7 1.0 concatenate.20
  2.8 1.0 concatenate.18
  3.8 0.1 maximum_bitcast_fusion
  4.0 0.3 reshape.67
  4.2 0.6 reshape.68.taps_row
  4.9 0.6 negate_sqrt_fusion
  5.5 0.0 copy-start.5
  5.5 0.6 fusion
  6.1 0.0 copy-done.1
  6.1 0.2 copy.24
  6.3 0.0 copy-done.2
  6.3 0.2 copy.25
  6.5 0.0 copy-done.3
  6.5 0.2 copy.26
  6.7 0.1 pad_maximum_fusion
  6.8 0.1 copy.27
  6.8 0.0 copy-done.5
  6.8 1.2 copy.28.x_ref
  8.0 40.9 %gather.1 = (bf16[4,3,128,256]{3,2,1,0:T(8,128)(2,1)}, bf16[4,128,4096]{2,1,0:T(8,128)(2,1)}, bf16[4,64,4096]{2,1,0:T(8,128)(2,1)}, bf16[3,16,256]{2,1,0:T(8,128)(2,1)}) custom-call(bf16[4,3,128,256]{3,2,1,0:T(8,128)(2,1)} %copy.28.x_ref, bf16[128,4096]{1,0:T(8,128)(2,1)} %bitcast.51, bf16[64,4096]{1,0:T(8,128)(2,1)} %w_ref.1), custom_call_target="tpu_custom_call" | custom-call | tf_op jit(solution)/shard_map/gather/pallas_call | solution.py:584
  49.0 0.0 copy-start.6
  49.0 0.9 slice_bitcast_fusion
  49.8 1.2 copy.29
  51.0 0.4 copy.30
  51.5 0.0 copy-done.6
  51.5 3.5 %fusion.2 = f32[8,64,256]{2,1,0:T(8,128)S(1)} fusion(bf16[8,64,4096]{2,1,0:T(8,128)(2,1)} %bitcast.42, bf16[256,4096,1]{1,0,2:T(8,128)(2,1)S(1)} %bitcast.61), kind=kOutput, calls=%fused_computation.12 | convolution fusion | flops 1073741824 | bytes 6815744 | tf_op jit(solution)/shard_map/dot_general | solution.py:605
  55.0 1.1 copy.47
  56.1 1.4 %convert_bitcast_fusion.x_ref = f32[3,72,8,256]{3,2,1,0:T(8,128)} fusion(bf16[3,8,64,256]{3,1,2,0:T(8,128)(2,1)S(1)} %copy.30, bf16[3,7,8,256]{3,1,2,0:T(8,128)(2,1)S(1)} %slice.66, bf16[3,1,8,256]{3,1,2,0:T(2,128)(2,1)S(1)} %copy.31), kind=kLoop, calls=%fused_computation | loop fusion | flops 2654208 | bytes 2654208 | tf_op jit(solution)/shard_map/convert_element_type | solution.py:616
  57.5 65.5 %scan.1 = (f32[64,4096]{1,0:T(8,128)}, bf16[4,3,128,256]{3,2,1,0:T(8,128)(2,1)}, f32[4,40,256]{2,1,0:T(8,128)}) custom-call(f32[3,72,8,256]{3,2,1,0:T(8,128)} %convert_bitcast_fusion.x_ref, f32[64,8,256]{2,1,0:T(8,128)} %bitcast.48, f32[3,7,256]{2,1,0:T(8,128)} %reshape.68.taps_row, f32[16,256]{1,0:T(8,128)} %get-tuple-element.32.factor_row, ...), custom_call_target="tpu_custom_call" | custom-call | tf_op jit(solution)/shard_map/scan/pallas_call | solution.py:633
  123.0 1.5 %copy.37 = bf16[4,3,128,256]{2,3,1,0:T(8,128)(2,1)S(1)} copy(bf16[4,3,128,256]{3,2,1,0:T(8,128)(2,1)} %get-tuple-element.17) | data formatting | bytes 1572864 | tf_op jit(solution)/shard_map/scan/pallas_call | solution.py:633
  124.5 0.0 copy-start.4
  124.5 0.1 fusion.1
  124.6 0.9 copy.45
  125.5 0.0 copy-start
  125.5 0.9 copy.44
  126.3 0.9 copy.43
  127.2 0.0 copy-done.4
  127.2 0.2 reshape.71
  127.5 0.8 reshape.72
  128.3 0.1 copy.42
  128.4 0.8 slice.65
  129.1 0.0 copy-done
  129.1 1.0 copy.49
  (12 shorter events, 0.3 us)
Async XLA Ops:
  0.6 5.7 %copy-start.2 = (bf16[1,128,1024]{2,1,0:T(8,128)(2,1)S(1)}, bf16[1,128,1024]{2,1,0:T(8,128)(2,1)}, u32[]{:S(2)}) copy-start(bf16[1,128,1024]{2,1,0:T(8,128)(2,1)} %param.9) | copy-start | bytes 786436
  0.6 5.5 %copy-start.1 = (bf16[1,128,1024]{2,1,0:T(8,128)(2,1)S(1)}, bf16[1,128,1024]{2,1,0:T(8,128)(2,1)}, u32[]{:S(2)}) copy-start(bf16[1,128,1024]{2,1,0:T(8,128)(2,1)} %param.8) | copy-start | bytes 786436
  1.7 4.8 %copy-start.3 = (bf16[1,128,1024]{2,1,0:T(8,128)(2,1)S(1)}, bf16[1,128,1024]{2,1,0:T(8,128)(2,1)}, u32[]{:S(2)}) copy-start(bf16[1,128,1024]{2,1,0:T(8,128)(2,1)} %param.10) | copy-start | bytes 786436
  5.5 1.3 %copy-start.5 = (f32[16,256]{1,0:T(8,128)}, f32[16,256]{1,0:T(8,128)S(1)}, u32[]{:S(2)}) copy-start(f32[16,256]{1,0:T(8,128)S(1)} %get-tuple-element.27.rate_row) | copy-start | bytes 49156
  49.0 2.5 %copy-start.6 = (bf16[4,64,4096]{2,1,0:T(8,128)(2,1)S(1)}, bf16[4,64,4096]{2,1,0:T(8,128)(2,1)}, u32[]{:S(2)}) copy-start(bf16[4,64,4096]{2,1,0:T(8,128)(2,1)} %get-tuple-element.16) | copy-start | bytes 6291460
  124.5 2.7 %copy-start.4 = (f32[4,40,256]{2,1,0:T(8,128)S(1)}, f32[4,40,256]{2,1,0:T(8,128)}, u32[]{:S(2)}) copy-start(f32[4,40,256]{2,1,0:T(8,128)} %get-tuple-element.19) | copy-start | bytes 491524
  125.5 3.7 %copy-start = (f32[64,4096]{1,0:T(8,128)S(1)}, f32[64,4096]{1,0:T(8,128)}, u32[]{:S(2)}) copy-start(f32[64,4096]{1,0:T(8,128)} %get-tuple-element.42) | copy-start | bytes 3145732
